TPU v7x, 512 devices: a whole 4x4x16 slice. The times are simulated.
512 devices in a mesh: tm: 16 (over y, x_lo, core), chan: 32 (over z, x_hi).
Axes of the slice: x: 4 (x_hi: 2, x_lo: 2; x = x_hi * 2 + x_lo), y: 4, z: 16, core: 2. Of those that a mesh axis runs over, the one named last changes fastest.
Arguments:
- raw: bfloat16 [16384, 4096], P('tm', 'chan'), may hold values from -6 to 6
- taps: bfloat16 [512], replicated, may hold values from -0.25 to 0.25
Outputs:
- correlations: float32 [4096, 64, 1024], P('chan', 'tm')
All inputs are finite; a program needn't handle non-finite values.
Results may differ from a plain program's by a relative error of at most 0.0044.
Values may be sent and summed in bfloat16 or wider, within the bound.
No kernel may reach another device: no remote copies, remote signals or barrier semaphores. Data moves between devices by JAX's collectives and lax.ppermute only.
A program may use at most 128 MiB of HBM per device.

v0:
```python
import math

import jax
import jax.numpy as jnp
from jax import lax
from jax.sharding import PartitionSpec as P

TAPS = 512
HW = 64
FR = 1024
SRC_DEV = 2
LAGS = 1024


epsilon = 1e-05


def shifted(block, axis, distance):
    devices = range(lax.axis_size(axis))
    route = [(i - distance, i) for i in devices if i - distance in devices]
    return lax.ppermute(block, axis, route)


def padded(array, sides, width):
    for axis, dim in sides:
        count, length = (lax.axis_size(axis), array.shape[dim])
        up = [(i, (i + 1) % count) for i in range(count - 1)]
        down = [(j, i) for i, j in up]
        last = lax.slice_in_dim(array, length - width, length, axis=dim)
        initial = lax.slice_in_dim(array, 0, width, axis=dim)
        before = lax.ppermute(last, axis, up)
        after = lax.ppermute(initial, axis, down)
        array = jnp.concatenate([before, array, after], axis=dim)
    return array


def forward_table(first, count):
    freq = first + jnp.arange(count, dtype=jnp.int32)
    sample = jnp.arange(FR, dtype=jnp.int32)
    phase = freq[:, None] * sample[None, :] % (2 * FR)
    angle = phase.astype(jnp.float32) * (math.pi / FR)
    return jnp.stack([jnp.cos(angle), -jnp.sin(angle)])


def inverse_table(first, count, scale):
    freq = first + jnp.arange(count, dtype=jnp.int32)
    lagged = jnp.arange(LAGS, dtype=jnp.int32) - LAGS // 2 + 2 * FR
    phase = freq[:, None] * lagged[None, :] % (2 * FR)
    angle = phase.astype(jnp.float32) * (math.pi / FR)
    weight = jnp.where(freq == 0, 1.0, 2.0).astype(jnp.float32) * (scale / (2 * FR))
    return jnp.stack([weight[:, None] * jnp.cos(angle), -weight[:, None] * jnp.sin(angle)])


def transform(frames32, pattern, axis_out):
    width = min(256, FR)
    pieces = []
    for first in range(0, FR, width):
        table = forward_table(first, width)
        pieces.append(jnp.einsum(pattern, table, frames32, precision=lax.Precision.HIGHEST))
    return jnp.concatenate(pieces, axis_out)


def correlate(cross, scale):
    width = min(256, FR)
    result = jnp.zeros(cross.shape[:2] + (LAGS,), jnp.float32)
    for first in range(0, FR, width):
        table = inverse_table(first, width, scale)
        result = result + jnp.einsum(
            "rkgf,gfl->rkl",
            cross[..., first : first + width],
            table,
            precision=lax.Precision.HIGHEST,
        )
    return result


def on_device(raw, taps):
    samples, channels = raw.shape
    time_parts = lax.axis_size("tm")
    chan_parts = lax.axis_size("chan")
    frames_dev = samples // FR
    frame_total = frames_dev * time_parts
    sources_total = SRC_DEV * chan_parts
    stride = channels // SRC_DEV
    scale = 1.0 / math.sqrt(frame_total * FR)
    kernel = jnp.broadcast_to(taps[:, None, None], (TAPS, 1, channels))
    before = shifted(raw[samples - TAPS + 1 :], "tm", 1)
    filtered = lax.conv_general_dilated(
        jnp.concatenate([before, raw], 0)[None],
        kernel,
        (1,),
        "VALID",
        dimension_numbers=("NWC", "WIO", "NWC"),
        feature_group_count=channels,
        preferred_element_type=jnp.float32,
    )[0]
    widened = padded(filtered, (("tm", 0),), HW)
    total = lax.reduce_window(
        jnp.abs(widened), jnp.zeros((), jnp.float32), lax.add, (2 * HW + 1, 1), (1, 1), "VALID"
    )
    level = total / (2 * HW + 1)
    whitened = (widened[HW : HW + samples] / (level + epsilon)).astype(jnp.bfloat16)
    frames32 = whitened.astype(jnp.float32).reshape(frames_dev, FR, channels)
    spectra = transform(frames32, "gft,btc->bgfc", 2).astype(jnp.bfloat16)
    banded = lax.all_to_all(spectra, "tm", split_axis=2, concat_axis=0, tiled=True)
    own_re = banded[:, 0]
    own_im = banded[:, 1]
    picked = banded[..., ::stride]
    band_width = banded.shape[2]
    empty = jnp.zeros((channels, sources_total, 2, band_width), jnp.float32)
    piece = lax.all_gather(picked, "chan", axis=3, tiled=True)
    piece_re = piece[:, 0]
    piece_im = piece[:, 1]
    real_part = jnp.einsum(
        "bfs,bfc->csf", piece_re, own_re, preferred_element_type=jnp.float32
    ) + jnp.einsum("bfs,bfc->csf", piece_im, own_im, preferred_element_type=jnp.float32)
    imag_part = jnp.einsum(
        "bfs,bfc->csf", piece_re, own_im, preferred_element_type=jnp.float32
    ) - jnp.einsum("bfs,bfc->csf", piece_im, own_re, preferred_element_type=jnp.float32)
    stacked = jnp.stack([real_part, imag_part], 2)
    cross = lax.dynamic_update_slice_in_dim(empty, stacked, jnp.int32(0), 1)
    return correlate(lax.all_to_all(cross, "tm", split_axis=1, concat_axis=3, tiled=True), scale)


def solution(mesh):
    placed = (P("tm", "chan"), P())
    return jax.shard_map(
        on_device, mesh=mesh, in_specs=placed, out_specs=P("chan", "tm", None), check_vma=False
    )
```

profile of v0, /device:TPU:1, one launch (start us, length us, event | category | flops | bytes accessed | tf_op | source)
XLA Modules:
  0.0 304.3 jit_solution(13636452753575318065)
XLA Ops:
  0.0 1.0 slice.42
  1.0 4.5 %collective-permute-start = (bf16[511,128]{1,0:T(8,128)(2,1)S(1)}, bf16[511,128]{1,0:T(8,128)(2,1)S(1)}, u32[]{:S(2)}, u32[]{:S(2)}) collective-permute-start(bf16[511,128]{1,0:T(8,128)(2,1)S(1)} %slice.42), channel_id=1, source_target_pairs={{0,32},{32,64},{64,96},{96,128},{128,160},{160,192},{192,224},{224... | collective-permute-start | bytes 392456 | tf_op jit(solution)/shard_map/ppermute | solution.py:21
  5.6 32.5 %cosine_multiply_fusion = (f32[1,256,1024]{2,1,0:T(8,128)}, f32[1,256,1024]{2,1,0:T(8,128)}, f32[1,256,1024]{2,1,0:T(8,128)}, f32[1,256,1024]{2,1,0:T(8,128)}, f...) fusion(f32[256]{0:T(256)S(1)} %get-tuple-element.30, ...), kind=kLoop, calls=%fused_computation.105 | loop fusion | flops 28573696 | bytes 14695424 | tf_op jit(solution)/shard_map/mul | solution.py:51
  38.1 0.6 fusion.132
  38.8 44.4 %fusion.95 = f32[1,1024,128]{2,0,1:T(1,128)S(1)} fusion(bf16[1,1535,128]{2,1,0:T(8,128)(2,1)S(1)} %maximum_bitcast_fusion.10, bf16[512,1,128]{2,1,0:T(2,128)(2,1)S(1)} %fusion.132), kind=kOutput, calls=%fused_computation.131 | convolution fusion | flops 134217728 | bytes 1048320 | tf_op jit(solution)/shard_map/conv_general_dilated | solution.py:88
  83.2 1.9 collective-permute-start.1
  85.1 4.9 %collective-permute-start.2 = (f32[64,128]{1,0:T(8,128)S(1)}, f32[64,128]{1,0:T(8,128)S(1)}, u32[]{:S(2)}, u32[]{:S(2)}) collective-permute-start(f32[64,128]{1,0:T(8,128)S(1)} %get-tuple-element.8), channel_id=1, source_target_pairs={{32,0},{64,32},{96,64},{128,96},{160,128},{192,160},{224,192},{256... | collective-permute-start | bytes 98312 | tf_op jit(solution)/shard_map/ppermute | solution.py:32
  90.1 4.1 %sine_negate_fusion.3 = (f32[1,256,1024]{2,1,0:T(8,128)S(1)}, f32[1,256,1024]{2,1,0:T(8,128)S(1)}) fusion(), kind=kLoop, calls=%fused_computation.123 | loop fusion | flops 3932160 | bytes 2097152 | tf_op jit(solution)/shard_map/neg | solution.py:42
  94.2 0.9 maximum_abs_fusion
  95.2 19.6 %reduce_window.7 = f32[1,1024,128]{2,1,0:T(8,128)} reduce-window(f32[1,1152,128]{2,1,0:T(8,128)} %maximum_abs_fusion, f32[]{:T(128)} %constant.65.clone.1), window={size=1x129x1}, to_apply=%region_0.0 | reduce-window | flops 16777216 | bytes 1114116 | tf_op jit(solution)/shard_map/reduce_window | solution.py:98
  114.8 1.4 divide_convert_fusion
  116.2 1.7 fusion.40
  118.0 1.3 fusion.46
  119.3 1.3 fusion.43
  120.6 1.3 fusion.49
  122.4 12.6 %all_to_all.36 = bf16[1,2,1024,128]{3,1,0,2:T(2,128)(2,1)S(1)} all-to-all(bf16[1,2,1024,128]{3,1,0,2:T(2,128)(2,1)S(1)} %copy.91), channel_id=1, replica_groups=mesh['tm'=16,'chan'=32] {'tm'}, dimensions={2} | all-to-all | bytes 1048576 | tf_op jit(solution)/shard_map/all_to_all | solution.py:105
  135.4 2.0 slice.48
  137.4 0.5 copy.94
  137.9 71.7 %all_gather.3 = bf16[16,2,64,64]{2,0,1,3:T(8,128)(2,1)S(1)} all-gather(bf16[16,2,64,2]{2,0,1,3:T(8,128)(2,1)S(1)} %copy.94), channel_id=1, replica_groups=mesh['tm'=16,'chan'=32] {'chan'}, dimensions={3}, use_global_device_ids=true | all-gather | bytes 270336 | tf_op jit(solution)/shard_map/all_gather | solution.py:111
  210.1 1.8 fusion.107
  212.8 2.1 subtract_bitcast_fusion
  214.9 0.5 add_bitcast_fusion
  215.4 0.6 pad_maximum_fusion
  215.9 2.4 copy.97
  218.4 66.6 %all_to_all.37 = f32[128,64,2,64]{0,3,2,1:T(8,128)S(1)} all-to-all(f32[128,64,2,64]{0,3,2,1:T(8,128)S(1)} %copy.97), channel_id=1, replica_groups=mesh['tm'=16,'chan'=32] {'tm'}, dimensions={1} | all-to-all | bytes 8388608 | tf_op jit(solution)/shard_map/all_to_all | solution.py:122
  285.0 0.6 copy.98
  285.6 0.6 copy-done.5
  286.6 3.5 %fusion.22 = f32[128,4,1024,1]{2,0,3,1:T(8,128)S(1)} fusion(f32[1,256,1024]{2,1,0:T(8,128)S(1)} %copy-done.5, f32[1,256,1024]{2,1,0:T(8,128)S(1)} %copy-done.6, f32[128,4,2,1024]{0,3,2,1:T(8,128)S(1)} %bitcast.109), kind=kOutput, calls=%fused_computation.26 | convolution fusion | flops 3221749760 | bytes 5242880 | tf_op jit(solution)/shard_map/rkgf,gfl->rkl/dot_general | solution.py:68
  290.2 3.6 %fusion.19 = f32[128,4,1024,1]{2,0,3,1:T(8,128)S(1)} fusion(f32[1,256,1024]{2,1,0:T(8,128)S(1)} %copy-done.3, f32[1,256,1024]{2,1,0:T(8,128)S(1)} %copy-done.4, f32[128,4,2,1024]{0,3,2,1:T(8,128)S(1)} %bitcast.110), kind=kOutput, calls=%fused_computation.22 | convolution fusion | flops 3221749760 | bytes 5242880 | tf_op jit(solution)/shard_map/rkgf,gfl->rkl/dot_general | solution.py:68
  293.8 3.6 %fusion.16 = f32[128,4,1024,1]{2,0,3,1:T(8,128)S(1)} fusion(f32[1,256,1024]{2,1,0:T(8,128)S(1)} %copy-done.1, f32[1,256,1024]{2,1,0:T(8,128)S(1)} %copy-done.2, f32[128,4,2,1024]{0,3,2,1:T(8,128)S(1)} %bitcast.111), kind=kOutput, calls=%fused_computation.18 | convolution fusion | flops 3221749760 | bytes 5242880 | tf_op jit(solution)/shard_map/rkgf,gfl->rkl/dot_general | solution.py:68
  297.3 4.1 %bitcast_add_fusion = f32[128,4,1024]{2,0,1:T(8,128)S(1)} fusion(f32[128,4,1024,1]{2,0,3,1:T(8,128)S(1)} %fusion.22, f32[128,4,1024,1]{2,0,3,1:T(8,128)S(1)} %fusion.19, f32[128,4,1024,1]{2,0,3,1:T(8,128)S(1)} %fusion.16, f32[1,256,1024]{2,1,0:T(8,128)S(1)} %copy-done.13, f32[1,256,1024]{2,1,0:T(8,128)S(1)} %copy-done.12, f32[128,4,2,1024]{0,3,2,1:T(8,128)S(1)} %bitcast.112), kind=kOutput, calls=%fused_computation.33 | convolution fusion | flops 3223322624 | bytes 11534336 | tf_op jit(solution)/shard_map/rkgf,gfl->rkl/dot_general | solution.py:68
  301.4 2.7 copy.103
  (50 shorter events, 2.6 us)
Async XLA Ops:
  0.0 38.1 %copy-start = (bf16[512]{0:T(512)(128)(2,1)S(1)}, bf16[512]{0:T(512)(128)(2,1)}, u32[]{:S(2)}) copy-start(bf16[512]{0:T(512)(128)(2,1)} %param.3) | copy-start | bytes 3076
  1.0 37.7 %collective-permute-start = (bf16[511,128]{1,0:T(8,128)(2,1)S(1)}, bf16[511,128]{1,0:T(8,128)(2,1)S(1)}, u32[]{:S(2)}, u32[]{:S(2)}) collective-permute-start(bf16[511,128]{1,0:T(8,128)(2,1)S(1)} %slice.42), channel_id=1, source_target_pairs={{0,32},{32,64},{64,96},{96,128},{128,160},{160,192},{192,224},{224... | collective-permute-start | bytes 392456 | tf_op jit(solution)/shard_map/ppermute | solution.py:21
  5.6 33.1 %copy-start.15 = (bf16[1024,128]{1,0:T(8,128)(2,1)S(1)}, bf16[1024,128]{1,0:T(8,128)(2,1)}, u32[]{:S(2)}) copy-start(bf16[1024,128]{1,0:T(8,128)(2,1)} %param.2) | copy-start | bytes 786436
  83.2 11.0 %copy-start.14 = (f32[1,1024,128]{2,0,1:T(1,128)}, f32[1,1024,128]{2,0,1:T(1,128)S(1)}, u32[]{:S(2)}) copy-start(f32[1,1024,128]{2,0,1:T(1,128)S(1)} %fusion.95) | copy-start | bytes 1572868
  83.2 11.0 %collective-permute-start.1 = (f32[64,128]{1,0:T(8,128)S(1)}, f32[64,128]{1,0:T(8,128)S(1)}, u32[]{:S(2)}, u32[]{:S(2)}) collective-permute-start(f32[64,128]{1,0:T(8,128)S(1)} %get-tuple-element.7), channel_id=1, source_target_pairs={{0,32},{32,64},{64,96},{96,128},{128,160},{160,192},{192,224},{224... | collective-permute-start | bytes 98312 | tf_op jit(solution)/shard_map/ppermute | solution.py:31
  85.1 9.1 %collective-permute-start.2 = (f32[64,128]{1,0:T(8,128)S(1)}, f32[64,128]{1,0:T(8,128)S(1)}, u32[]{:S(2)}, u32[]{:S(2)}) collective-permute-start(f32[64,128]{1,0:T(8,128)S(1)} %get-tuple-element.8), channel_id=1, source_target_pairs={{32,0},{64,32},{96,64},{128,96},{160,128},{192,160},{224,192},{256... | collective-permute-start | bytes 98312 | tf_op jit(solution)/shard_map/ppermute | solution.py:32
  114.8 3.2 %copy-start.10 = (f32[1,256,1024]{2,1,0:T(8,128)S(1)}, f32[1,256,1024]{2,1,0:T(8,128)}, u32[]{:S(2)}) copy-start(f32[1,256,1024]{2,1,0:T(8,128)} %get-tuple-element.21) | copy-start | bytes 3145732
  114.8 3.2 %copy-start.11 = (f32[1,256,1024]{2,1,0:T(8,128)S(1)}, f32[1,256,1024]{2,1,0:T(8,128)}, u32[]{:S(2)}) copy-start(f32[1,256,1024]{2,1,0:T(8,128)} %get-tuple-element.22) | copy-start | bytes 3145732
  116.2 3.1 %copy-start.8 = (f32[1,256,1024]{2,1,0:T(8,128)S(1)}, f32[1,256,1024]{2,1,0:T(8,128)}, u32[]{:S(2)}) copy-start(f32[1,256,1024]{2,1,0:T(8,128)} %get-tuple-element.23) | copy-start | bytes 3145732
  116.2 3.1 %copy-start.9 = (f32[1,256,1024]{2,1,0:T(8,128)S(1)}, f32[1,256,1024]{2,1,0:T(8,128)}, u32[]{:S(2)}) copy-start(f32[1,256,1024]{2,1,0:T(8,128)} %get-tuple-element.24) | copy-start | bytes 3145732
  118.0 2.7 copy-start.7
  285.0 1.2 copy-start.5
  285.0 1.5 copy-start.6
  286.6 3.6 %copy-start.3 = (f32[1,256,1024]{2,1,0:T(8,128)S(1)}, f32[1,256,1024]{2,1,0:T(8,128)}, u32[]{:S(2)}) copy-start(f32[1,256,1024]{2,1,0:T(8,128)} %get-tuple-element.16) | copy-start | bytes 3145732
  286.6 3.6 %copy-start.4 = (f32[1,256,1024]{2,1,0:T(8,128)S(1)}, f32[1,256,1024]{2,1,0:T(8,128)}, u32[]{:S(2)}) copy-start(f32[1,256,1024]{2,1,0:T(8,128)} %get-tuple-element.17) | copy-start | bytes 3145732
  290.1 3.6 %copy-start.1 = (f32[1,256,1024]{2,1,0:T(8,128)S(1)}, f32[1,256,1024]{2,1,0:T(8,128)}, u32[]{:S(2)}) copy-start(f32[1,256,1024]{2,1,0:T(8,128)} %get-tuple-element.15) | copy-start | bytes 3145732
  290.1 3.6 %copy-start.2 = (f32[1,256,1024]{2,1,0:T(8,128)S(1)}, f32[1,256,1024]{2,1,0:T(8,128)}, u32[]{:S(2)}) copy-start(f32[1,256,1024]{2,1,0:T(8,128)} %get-tuple-element.20) | copy-start | bytes 3145732
  293.7 3.6 %copy-start.12 = (f32[1,256,1024]{2,1,0:T(8,128)S(1)}, f32[1,256,1024]{2,1,0:T(8,128)}, u32[]{:S(2)}) copy-start(f32[1,256,1024]{2,1,0:T(8,128)} %get-tuple-element.9) | copy-start | bytes 3145732
  293.7 3.6 %copy-start.13 = (f32[1,256,1024]{2,1,0:T(8,128)S(1)}, f32[1,256,1024]{2,1,0:T(8,128)}, u32[]{:S(2)}) copy-start(f32[1,256,1024]{2,1,0:T(8,128)} %get-tuple-element.10) | copy-start | bytes 3145732
where the time goes:
time: 307 us; the launch traced here: 304 us
  blocking collectives  151 us (49%)
  matrix products  69.7 us (23%)
  other arithmetic  59.3 us (19%)
  local copies, waits for them, and re-layouts  12.3 us (4%)
  starting transfers between devices  11.4 us (4%)
    all_gather x1, blocking collectives, on_device(): piece = lax.all_gather(picked, 'chan', axis=3, tiled=True)  71.7 us
    all_to_all x1, blocking collectives, on_device(): lax.all_to_all(cross, 'tm', split_axis=1, concat_axis=3, tiled=True)  66.6 us
    conv_general_dilated x1, matrix products, on_device(): lax.conv_general_dilated(jnp.concatenate([before, raw], 0)[None], kernel,...  44.4 us
    mul x1, other arithmetic, inverse_table(): weight[:, None] * jnp.cos(angle)  32.5 us
    another operation x1, other arithmetic, on_device(): lax.reduce_window(jnp.abs(widened), jnp.zeros((), jnp.float32), lax.add,...  19.6 us
    dot_general x4, matrix products, correlate(): jnp.einsum('rkgf,gfl->rkl', cross[..., first:first + width], table, preci...  14.8 us
    all_to_all x1, blocking collectives, on_device(): lax.all_to_all(spectra, 'tm', split_axis=2, concat_axis=0, tiled=True)  12.6 us
  transfers between devices with their start and end apart: 3, of which 0 were waited for; matrix products, arithmetic and copies ran while one was open for 12% of the time, Pallas kernels for 0%

commit v1 on v0

v1 whole, which is shorter than its diff:
```python
import functools
import math

import jax
import jax.numpy as jnp
from jax import lax
from jax.experimental import pallas as pl
from jax.experimental.pallas import tpu as pltpu
from jax.sharding import PartitionSpec as P

TAPS = 512
HW = 64
FR = 1024
LAGS = 1024
SRC_DEV = 2
BEFORE = 640
AFTER = 128
TILE = 256
EPS = 1e-05
BF16 = jnp.bfloat16
F32 = jnp.float32


def dot(a, b):
    return jnp.dot(a, b, preferred_element_type=F32)


def strip(row, first, store):
    width = row.shape[1]
    base = pltpu.roll(jnp.broadcast_to(row, (8, width)), first, 1, stride=1, stride_axis=0)
    for h in range(8):
        low = pltpu.roll(base, 16 * h, 1) if h else base
        high = pltpu.roll(base, 16 * h + 8, 1)
        store(h, jnp.concatenate([low, high], 0).astype(BF16))


def whiten_kernel(
    last_ref, before_ref, raw_ref, after_ref, taps_ref, white_ref, src_ref, toep_ref, rawt_ref, filt_ref
):
    channels = raw_ref.shape[1]
    toep_rows = TAPS + TILE

    def store(h, rows):
        for a in range(toep_rows // 128):
            at = BEFORE - 128 * a
            toep_ref[128 * a + 16 * h : 128 * a + 16 * h + 16, :] = rows[:, at : at + TILE]

    strip(taps_ref[...], 0, store)
    rawt_ref[:, :BEFORE] = before_ref[...].T
    rawt_ref[:, BEFORE : BEFORE + FR] = raw_ref[...].T
    rawt_ref[:, BEFORE + FR :] = after_ref[...].T
    toep = toep_ref[...]
    span = FR + 2 * AFTER
    for y in range(0, span, TILE):
        filt_ref[:, y : y + TILE] = dot(rawt_ref[:, y : y + toep_rows], toep)
    past = lax.broadcasted_iota(jnp.int32, (channels, AFTER), 0) * 0 + last_ref[0]
    filt_ref[:, span - AFTER :] = jnp.where(past == 1, 0.0, filt_ref[:, span - AFTER :])
    size = jnp.abs(filt_ref[...])
    hi = size.astype(BF16)
    lo = (size - hi.astype(F32)).astype(BF16)
    gap = lax.broadcasted_iota(jnp.int32, (2 * TILE, TILE), 0) - lax.broadcasted_iota(
        jnp.int32, (2 * TILE, TILE), 1
    )
    band = jnp.where((gap >= AFTER - HW) & (gap <= AFTER + HW), 1.0, 0.0).astype(BF16)
    stride = channels // SRC_DEV
    row = lax.broadcasted_iota(jnp.int32, (16, channels), 0)
    col = lax.broadcasted_iota(jnp.int32, (16, channels), 1)
    pick = jnp.where((col == row * stride) & (row < SRC_DEV), 1.0, 0.0).astype(BF16)
    r = lax.broadcasted_iota(jnp.int32, (128, 128), 0)
    c = lax.broadcasted_iota(jnp.int32, (128, 128), 1)
    flip = jnp.where(r + c == 127, 1.0, 0.0).astype(BF16)
    for t in range(0, FR, TILE):
        total = dot(hi[:, t : t + 2 * TILE], band) + dot(lo[:, t : t + 2 * TILE], band)
        level = total / (2 * HW + 1)
        center = filt_ref[:, AFTER + t : AFTER + t + TILE]
        white = (center / (level + EPS)).astype(BF16)
        for u in range(0, TILE, 128):
            q = (t + u) // 128
            part = white[:, u : u + 128]
            white_ref[channels * q : channels * (q + 1), :] = part
            back = dot(dot(pick, part).astype(BF16), flip).astype(BF16)
            for k in range(SRC_DEV):
                at = k * (FR // 128) + FR // 128 - 1 - q
                src_ref[at : at + 1, :] = back[k : k + 1]


def correlate_kernel(
    base_ref, white_ref, src_ref, out_ref, lhs_ref, nyq_ref, toep0_ref, toep1_ref, acc_ref, *, scale
):
    frames = white_ref.shape[0]
    count, channels, _ = out_ref.shape
    blocks = FR // TILE
    toeps = (toep0_ref, toep1_ref)
    pad = jnp.zeros((1, TILE), F32)

    def build(s):
        to_ref = toeps[s % 2]
        own = src_ref[s]
        for b in range(frames):

            def store(h, rows, b=b):
                at = TILE * b + 16 * h
                to_ref[at : at + 16, :] = rows[:, TILE:]
                to_ref[at + 128 : at + 144, :] = rows[:, TILE - 128 : -128]

            strip(jnp.concatenate([pad, own[b : b + 1], pad], 1), 1, store)

    sign = 1.0 - 2.0 * (lax.broadcasted_iota(jnp.int32, (128, 128), 0) % 2).astype(F32)
    alternate = sign.astype(BF16)
    build(0)
    for b in range(frames):
        nyq = jnp.zeros((channels, 128), F32)
        for q in range(FR // 128):
            part = white_ref[b, channels * q : channels * (q + 1), :]
            to = channels * (q // 2)
            at = TILE * b + 128 * (q % 2)
            lhs_ref[to : to + channels, at : at + 128] = part
            nyq += dot(part, alternate)
        nyq_ref[b] = nyq

    for s in range(count):
        if s + 1 < count:
            build(s + 1)
        toep_ref = toeps[s % 2]
        for d in (0, 1, -1, 2, -2):
            at = TILE * (2 - d)
            first = channels * max(d, 0)
            rows = channels * (blocks - abs(d))
            res = dot(lhs_ref[first : first + rows, :], toep_ref[:, at : at + TILE])
            to = channels * max(-d, 0)
            if d == 0:
                acc_ref[...] = res
            else:
                acc_ref[to : to + rows, :] += res

        own = src_ref[s]
        lane = lax.broadcasted_iota(jnp.int32, (frames, FR), 1)
        own_nyq = jnp.sum(jnp.where(lane % 2 == 1, own, -own), axis=1, keepdims=True)
        nyq = own_nyq[0:1] * nyq_ref[0]
        for b in range(1, frames):
            nyq += own_nyq[b : b + 1] * nyq_ref[b]
        lane = lax.broadcasted_iota(jnp.int32, (channels, 128), 1)
        nyq = jnp.where(lane % 2 == 1, -nyq, nyq) * (scale / (2 * FR))
        nyq = jnp.concatenate([nyq] * (TILE // 128), 1)
        for j in range(blocks):
            part = acc_ref[channels * j : channels * (j + 1), :] * scale - nyq
            out_ref[s, :, TILE * j : TILE * (j + 1)] = part.astype(out_ref.dtype)


def correlate(base, bundle, src, channels, count, scale, dtype):
    frames = bundle.shape[0]
    rows = channels * (FR // 128)
    return pl.pallas_call(
        functools.partial(correlate_kernel, scale=scale),
        out_shape=jax.ShapeDtypeStruct((count, channels, LAGS), dtype),
        grid_spec=pltpu.PrefetchScalarGridSpec(
            num_scalar_prefetch=1,
            grid=(1,),
            in_specs=[
                pl.BlockSpec((frames, rows, 128), lambda i, base: (0, 0, 0)),
                pl.BlockSpec((count, frames, FR), lambda i, base: (base[0], 0, 0)),
            ],
            out_specs=pl.BlockSpec((count, channels, LAGS), lambda i, base: (0, 0, 0)),
            scratch_shapes=[
                pltpu.VMEM((FR // TILE * channels, TILE * frames), BF16),
                pltpu.VMEM((frames, channels, 128), F32),
                pltpu.VMEM((TILE * frames, 5 * TILE), BF16),
                pltpu.VMEM((TILE * frames, 5 * TILE), BF16),
                pltpu.VMEM((FR // TILE * channels, TILE), F32),
            ],
        ),
        compiler_params=pltpu.CompilerParams(vmem_limit_bytes=50 << 20),
    )(base, bundle, src)


def finish_kernel(ours_ref, theirs_ref, out_ref):
    count, channels, _ = ours_ref.shape
    for s in range(count):
        for q in range(LAGS // 128):
            lanes = slice(128 * q, 128 * (q + 1))
            both = ours_ref[s, :, lanes] + theirs_ref[s, :, lanes].astype(F32)
            out_ref[pl.ds(count * q + s, channels, stride=count * LAGS // 128), :] = both


def finish(ours, theirs):
    count, channels, _ = ours.shape
    out = pl.pallas_call(
        finish_kernel,
        out_shape=jax.ShapeDtypeStruct((channels * LAGS // 128 * count, 128), F32),
        compiler_params=pltpu.CompilerParams(vmem_limit_bytes=50 << 20),
    )(ours, theirs)
    out = out.reshape(channels, LAGS // 128, count, 128).transpose(0, 2, 1, 3)
    return out.reshape(channels, count, LAGS)


def on_device(raw, taps):
    samples, channels = raw.shape
    time_parts = lax.axis_size("tm")
    chan_parts = lax.axis_size("chan")
    chips = time_parts // 2
    place = lax.axis_index("tm")
    core = place % 2
    sources = SRC_DEV * chan_parts // chips
    scale = 1.0 / math.sqrt(samples * time_parts)
    up = [(i, i + 1) for i in range(time_parts - 1)]
    down = [(i + 1, i) for i in range(time_parts - 1)]
    before = lax.ppermute(raw[samples - BEFORE :], "tm", up)
    after = lax.ppermute(raw[:AFTER], "tm", down)
    last = (place == time_parts - 1).astype(jnp.int32).reshape(1)
    taps_row = jnp.concatenate(
        [jnp.zeros((128,), F32), taps[::-1].astype(F32), jnp.zeros((384,), F32)]
    )[None]
    frame_rows = FR // 128
    whole = pl.BlockSpec(memory_space=pltpu.VMEM)
    white, src = pl.pallas_call(
        whiten_kernel,
        out_shape=(
            jax.ShapeDtypeStruct((frame_rows * channels, 128), BF16),
            jax.ShapeDtypeStruct((SRC_DEV * frame_rows, 128), BF16),
        ),
        in_specs=[pl.BlockSpec(memory_space=pltpu.SMEM), whole, whole, whole, whole],
        scratch_shapes=[
            pltpu.VMEM((TAPS + TILE, TILE), BF16),
            pltpu.VMEM((channels, BEFORE + FR + AFTER), BF16),
            pltpu.VMEM((channels, FR + 2 * AFTER), F32),
        ],
        compiler_params=pltpu.CompilerParams(vmem_limit_bytes=50 << 20),
    )(last, before, raw, after, taps_row)
    every = lax.all_to_all(
        jnp.broadcast_to(src[None], (chan_parts,) + src.shape), "chan", 0, 0, tiled=True
    )
    every = every.reshape(chips, sources * frame_rows, 128)
    bundle = jnp.concatenate([jnp.broadcast_to(white[None], (chips,) + white.shape), every], 1)
    groups = [[c + 2 * i for i in range(chips)] for c in range(2)]
    bundle = lax.all_to_all(bundle, "tm", 0, 0, tiled=True, axis_index_groups=groups)
    srcs = bundle[:, frame_rows * channels :].astype(F32)
    srcs = srcs.reshape(chips, sources, FR).transpose(1, 0, 2)
    half = sources // 2
    theirs = correlate((1 - core).reshape(1), bundle, srcs, channels, half, scale, BF16)
    theirs = lax.ppermute(theirs, "tm", [(i, i ^ 1) for i in range(time_parts)])
    ours = correlate(core.reshape(1), bundle, srcs, channels, half, scale, F32)
    return finish(ours, theirs)


def solution(mesh):
    placed = (P("tm", "chan"), P())
    return jax.shard_map(
        on_device, mesh=mesh, in_specs=placed, out_specs=P("chan", "tm", None), check_vma=False
    )
```

time: 307 us -> 111 us (0.36)
  blocking collectives: 151 us -> 32.4 us
  matrix products: 69.7 us -> 0 us
  other arithmetic: 59.3 us -> 1.56 us
  waiting for transfers between devices: 0.01 us -> 27.6 us
  Pallas kernels: 0 us -> 25.3 us
  local copies, waits for them, and re-layouts: 12.3 us -> 3.93 us
  starting transfers between devices: 11.4 us -> 19.5 us
    all_gather x1 -> x0, blocking collectives: 71.7 us -> none  [on_device(): piece = lax.all_gather(picked, 'chan', axis=3, tiled=True)]
    all_to_all x2 -> x1, blocking collectives: 79.2 us -> 32.4 us  [on_device(): lax.all_to_all(jnp.broadcast_to(src[None], (chan_parts,) + src.shape), 'c...]
    conv_general_dilated x1 -> x0, matrix products: 44.4 us -> none  [on_device(): lax.conv_general_dilated(jnp.concatenate([before, raw], 0)[None], kernel,...]
    mul x3 -> x0, other arithmetic: 32.5 us -> none  [the longest x1 32.5 us: inverse_table(): weight[:, None] * jnp.cos(angle)]
    all_to_all x0 -> x1, waiting for transfers between devices: none -> 27.5 us  [on_device(): lax.all_to_all(bundle, 'tm', 0, 0, tiled=True, axis_index_groups=groups)]
    pallas_call x0 -> x4, Pallas kernels: none -> 25.3 us  [the longest x2 19.5 us: correlate(): pl.pallas_call(functools.partial(correlate_kernel, scale=scale), out_shap...]
    dot_general x12 -> x0, matrix products: 25.3 us -> none  [the longest x4 14.8 us: correlate(): jnp.einsum('rkgf,gfl->rkl', cross[..., first:first + width], table, preci...]
    another operation x2 -> x0, other arithmetic: 20.2 us -> none  [the longest x1 19.6 us: on_device(): lax.reduce_window(jnp.abs(widened), jnp.zeros((), jnp.float32), lax.add,...]
  transfers between devices with their start and end apart: 3 -> 4, of which waited for: 0 -> 1; matrix products, arithmetic and copies ran while one was open for 12% -> 1% of each run, Pallas kernels for 0% -> 9%
where the time goes in v1:
time: 111 us; the launch traced here: 110 us
  blocking collectives  32.4 us (29%)
  waiting for transfers between devices  27.6 us (25%)
  Pallas kernels  25.3 us (23%)
  starting transfers between devices  19.5 us (18%)
  local copies, waits for them, and re-layouts  3.93 us (4%)
  other arithmetic  1.56 us (1%)
    all_to_all x1, blocking collectives, on_device(): lax.all_to_all(jnp.broadcast_to(src[None], (chan_parts,) + src.shape), 'c...  32.4 us
    all_to_all x1, waiting for transfers between devices, on_device(): lax.all_to_all(bundle, 'tm', 0, 0, tiled=True, axis_index_groups=groups)  27.5 us
    pallas_call x2, Pallas kernels, correlate(): pl.pallas_call(functools.partial(correlate_kernel, scale=scale), out_shap...  19.5 us
    ppermute x1, starting transfers between devices, on_device(): after = lax.ppermute(raw[:AFTER], 'tm', down)  5.56 us
    all_to_all x1, starting transfers between devices, on_device(): lax.all_to_all(bundle, 'tm', 0, 0, tiled=True, axis_index_groups=groups)  5.5 us
    ppermute x1, starting transfers between devices, on_device(): before = lax.ppermute(raw[samples - BEFORE:], 'tm', up)  4.51 us
    ppermute x1, starting transfers between devices, on_device(): theirs = lax.ppermute(theirs, 'tm', [(i, i ^ 1) for i in range(time_parts)])  3.89 us
    pallas_call x1, Pallas kernels, finish(): pl.pallas_call(finish_kernel, out_shape=jax.ShapeDtypeStruct((channels *...  3.42 us
  transfers between devices with their start and end apart: 4, of which 1 were waited for; matrix products, arithmetic and copies ran while one was open for 1% of the time, Pallas kernels for 9%

profile of v1, /device:TPU:1, one launch (start us, length us, event | category | flops | bytes accessed | tf_op | source)
XLA Modules:
  0.0 110.3 jit_solution(71184281861071712)
XLA Ops:
  0.0 0.9 slice.9
  0.9 4.5 %collective-permute-start = (bf16[640,128]{1,0:T(8,128)(2,1)S(1)}, bf16[640,128]{1,0:T(8,128)(2,1)S(1)}, u32[]{:S(2)}, u32[]{:S(2)}) collective-permute-start(bf16[640,128]{1,0:T(8,128)(2,1)S(1)} %slice.9), channel_id=1, source_target_pairs={{0,32},{32,64},{64,96},{96,128},{128,160},{160,192},{192,224},{224... | collective-permute-start | bytes 491528 | tf_op jit(solution)/shard_map/ppermute | solution.py:207
  5.4 0.8 slice.10
  6.2 5.6 %collective-permute-start.1 = (bf16[128,128]{1,0:T(8,128)(2,1)S(1)}, bf16[128,128]{1,0:T(8,128)(2,1)S(1)}, u32[]{:S(2)}, u32[]{:S(2)}) collective-permute-start(bf16[128,128]{1,0:T(8,128)(2,1)S(1)} %slice.10), channel_id=1, source_target_pairs={{32,0},{64,32},{96,64},{128,96},{160,128},{192,160},{224,192},{256... | collective-permute-start | bytes 98312 | tf_op jit(solution)/shard_map/ppermute | solution.py:208
  11.8 0.8 rev.3
  12.6 0.0 collective-permute-done.1.after_ref
  12.6 0.0 collective-permute-done.before_ref
  12.6 0.0 copy-start.1
  12.6 0.9 copy-done.1
  13.6 2.3 %shard_map.28 = (bf16[1024,128]{1,0:T(8,128)(2,1)S(1)}, bf16[16,128]{1,0:T(8,128)(2,1)S(1)}) custom-call(s32[1]{0:T(128)} %bitcast.1.last_ref, bf16[640,128]{1,0:T(8,128)(2,1)S(1)} %collective-permute-done.before_ref, bf16[1024,128]{1,0:T(8,128)(2,1)S(1)} %copy-done.1, bf16[128,128]{1,0:T(8,128)(2,1)S(1)} %collective-permute-done.1.after_ref, ...), custom_call_target="tpu_custom_call" | custom-call | tf_op jit(solution)/shard_map/pallas_call | solution.py:215
  16.0 32.4 %all_to_all.10 = bf16[32,16,128]{2,1,0:T(8,128)(2,1)S(1)} all-to-all(bf16[32,16,128]{2,1,0:T(8,128)(2,1)S(1)} %broadcast_in_dim.25), channel_id=1, replica_groups=mesh['tm'=16,'chan'=32] {'chan'}, dimensions={0} | all-to-all | bytes 262144 | tf_op jit(solution)/shard_map/all_to_all | solution.py:229
  48.4 0.3 broadcast_in_dim.24
  48.6 1.5 %pad_maximum_fusion = bf16[8,1088,128]{2,1,0:T(8,128)(2,1)} fusion(bf16[8,64,128]{2,1,0:T(8,128)(2,1)S(1)} %bitcast.16, bf16[8,1024,128]{2,1,0:T(8,128)(2,1)S(1)} %broadcast_in_dim.24), kind=kLoop, calls=%fused_computation | loop fusion | flops 4456448 | bytes 4456448 | tf_op jit(solution)/shard_map/concatenate | solution.py:233
  50.2 5.5 %all-to-all-start.1 = ((bf16[8,1088,128]{2,1,0:T(8,128)(2,1)}), bf16[8,1088,128]{2,1,0:T(8,128)(2,1)S(1)}, u32[]{:S(2)}, u32[]{:S(2)}) async-start(bf16[8,1088,128]{2,1,0:T(8,128)(2,1)} %pad_maximum_fusion), calls=%async_computation.1 | async-start | bytes 4456448 | tf_op jit(solution)/shard_map/all_to_all | solution.py:235
  55.7 27.5 %all-to-all-done.1.white_ref = bf16[8,1088,128]{2,1,0:T(8,128)(2,1)S(1)} async-done(((bf16[8,1088,128]{2,1,0:T(8,128)(2,1)}), bf16[8,1088,128]{2,1,0:T(8,128)(2,1)S(1)}, u32[]{:S(2)}, u32[]{:S(2)}) %all-to-all-start.1) | async-done | bytes 2228256 | tf_op jit(solution)/shard_map/all_to_all | solution.py:235
  83.2 0.0 copy-start
  83.3 0.2 copy.7
  83.4 9.1 %shard_map.30 = bf16[4,128,1024]{2,1,0:T(8,128)(2,1)S(1)} custom-call(s32[1]{0:T(128)} %bitcast.5.base_ref, bf16[8,1088,128]{2,1,0:T(8,128)(2,1)S(1)} %all-to-all-done.1.white_ref, f32[8,8,1024]{2,1,0:T(8,128)S(1)} %bitcast.13), custom_call_target="tpu_custom_call" | custom-call | tf_op jit(solution)/shard_map/pallas_call | solution.py:153
  92.6 0.0 copy-done
  92.6 3.9 %collective-permute-start.2 = (bf16[4,128,1024]{2,1,0:T(8,128)(2,1)S(1)}, bf16[4,128,1024]{2,1,0:T(8,128)(2,1)S(1)}, u32[]{:S(2)}, u32[]{:S(2)}) collective-permute-start(bf16[4,128,1024]{2,1,0:T(8,128)(2,1)S(1)} %shard_map.30), channel_id=1, source_target_pairs={{0,32},{32,0},{64,96},{96,64},{128,160},{160,128},{192,224},{224,1... | collective-permute-start | bytes 3145736 | tf_op jit(solution)/shard_map/ppermute | solution.py:240
  96.5 10.4 %shard_map.29.ours_ref = f32[4,128,1024]{2,1,0:T(8,128)S(1)} custom-call(s32[1]{0:T(128)} %bitcast.base_ref, bf16[8,1088,128]{2,1,0:T(8,128)(2,1)} %copy-done, f32[8,8,1024]{2,1,0:T(8,128)S(1)} %bitcast.14), custom_call_target="tpu_custom_call" | custom-call | tf_op jit(solution)/shard_map/pallas_call | solution.py:153
  106.9 0.0 collective-permute-done.2.theirs_ref
  106.9 3.4 %shard_map.31 = f32[4096,128]{1,0:T(8,128)} custom-call(f32[4,128,1024]{2,1,0:T(8,128)S(1)} %shard_map.29.ours_ref, bf16[4,128,1024]{2,1,0:T(8,128)(2,1)S(1)} %collective-permute-done.2.theirs_ref), custom_call_target="tpu_custom_call" | custom-call | tf_op jit(solution)/shard_map/pallas_call | solution.py:187
  (7 shorter events, 0.1 us)
Async XLA Ops:
  0.9 11.7 %collective-permute-start = (bf16[640,128]{1,0:T(8,128)(2,1)S(1)}, bf16[640,128]{1,0:T(8,128)(2,1)S(1)}, u32[]{:S(2)}, u32[]{:S(2)}) collective-permute-start(bf16[640,128]{1,0:T(8,128)(2,1)S(1)} %slice.9), channel_id=1, source_target_pairs={{0,32},{32,64},{64,96},{96,128},{128,160},{160,192},{192,224},{224... | collective-permute-start | bytes 491528 | tf_op jit(solution)/shard_map/ppermute | solution.py:207
  6.2 6.4 %collective-permute-start.1 = (bf16[128,128]{1,0:T(8,128)(2,1)S(1)}, bf16[128,128]{1,0:T(8,128)(2,1)S(1)}, u32[]{:S(2)}, u32[]{:S(2)}) collective-permute-start(bf16[128,128]{1,0:T(8,128)(2,1)S(1)} %slice.10), channel_id=1, source_target_pairs={{32,0},{64,32},{96,64},{128,96},{160,128},{192,160},{224,192},{256... | collective-permute-start | bytes 98312 | tf_op jit(solution)/shard_map/ppermute | solution.py:208
  12.6 1.0 copy-start.1
  50.2 33.0 %all-to-all-start.1 = ((bf16[8,1088,128]{2,1,0:T(8,128)(2,1)}), bf16[8,1088,128]{2,1,0:T(8,128)(2,1)S(1)}, u32[]{:S(2)}, u32[]{:S(2)}) async-start(bf16[8,1088,128]{2,1,0:T(8,128)(2,1)} %pad_maximum_fusion), calls=%async_computation.1 | async-start | bytes 4456448 | tf_op jit(solution)/shard_map/all_to_all | solution.py:235
  83.2 9.4 %copy-start = (bf16[8,1088,128]{2,1,0:T(8,128)(2,1)}, bf16[8,1088,128]{2,1,0:T(8,128)(2,1)S(1)}, u32[]{:S(2)}) copy-start(bf16[8,1088,128]{2,1,0:T(8,128)(2,1)S(1)} %all-to-all-done.1.white_ref) | copy-start | bytes 6684676
  92.6 14.3 %collective-permute-start.2 = (bf16[4,128,1024]{2,1,0:T(8,128)(2,1)S(1)}, bf16[4,128,1024]{2,1,0:T(8,128)(2,1)S(1)}, u32[]{:S(2)}, u32[]{:S(2)}) collective-permute-start(bf16[4,128,1024]{2,1,0:T(8,128)(2,1)S(1)} %shard_map.30), channel_id=1, source_target_pairs={{0,32},{32,0},{64,96},{96,64},{128,160},{160,128},{192,224},{224,1... | collective-permute-start | bytes 3145736 | tf_op jit(solution)/shard_map/ppermute | solution.py:240

commit v2 on v1

v2 whole, which is shorter than its diff:
```python
import functools
import math

import jax
import jax.numpy as jnp
from jax import lax
from jax.experimental import pallas as pl
from jax.experimental.pallas import tpu as pltpu
from jax.sharding import PartitionSpec as P

TAPS = 512
HW = 64
FR = 1024
LAGS = 1024
SRC_DEV = 2
BEFORE = 640
AFTER = 128
TILE = 256
EPS = 1e-05
BF16 = jnp.bfloat16
F32 = jnp.float32


def dot(a, b):
    return jnp.dot(a, b, preferred_element_type=F32)


def strip(row, first, store):
    width = row.shape[1]
    base = pltpu.roll(jnp.broadcast_to(row, (8, width)), first, 1, stride=1, stride_axis=0)
    for h in range(8):
        low = pltpu.roll(base, 16 * h, 1) if h else base
        high = pltpu.roll(base, 16 * h + 8, 1)
        store(h, jnp.concatenate([low, high], 0).astype(BF16))


def whiten_kernel(
    last_ref, before_ref, raw_ref, after_ref, taps_ref, white_ref, src_ref, toep_ref, rawt_ref, filt_ref
):
    channels = raw_ref.shape[1]
    toep_rows = TAPS + TILE
    r = lax.broadcasted_iota(jnp.int32, (128, 128), 0)
    c = lax.broadcasted_iota(jnp.int32, (128, 128), 1)
    flip = jnp.where(r + c == 127, 1.0, 0.0).astype(BF16)
    taps = jnp.broadcast_to(taps_ref[...].astype(F32), (16, TAPS)).astype(BF16)
    parts = [jnp.zeros((1, 128), F32)]
    parts += [dot(taps[:, t - 128 : t], flip)[:1] for t in range(TAPS, 0, -128)]
    parts += [jnp.zeros((1, 384), F32)]

    def store(h, rows):
        for a in range(toep_rows // 128):
            at = BEFORE - 128 * a
            toep_ref[128 * a + 16 * h : 128 * a + 16 * h + 16, :] = rows[:, at : at + TILE]

    strip(jnp.concatenate(parts, 1), 0, store)
    rawt_ref[:, :BEFORE] = before_ref[FR - BEFORE :, :].T
    rawt_ref[:, BEFORE : BEFORE + FR] = raw_ref[...].T
    rawt_ref[:, BEFORE + FR :] = after_ref[...].T
    toep = toep_ref[...]
    span = FR + 2 * AFTER
    for y in range(0, span, TILE):
        filt_ref[:, y : y + TILE] = dot(rawt_ref[:, y : y + toep_rows], toep)
    past = lax.broadcasted_iota(jnp.int32, (channels, AFTER), 0) * 0 + last_ref[0]
    filt_ref[:, span - AFTER :] = jnp.where(past == 1, 0.0, filt_ref[:, span - AFTER :])
    size = jnp.abs(filt_ref[...])
    hi = size.astype(BF16)
    lo = (size - hi.astype(F32)).astype(BF16)
    gap = lax.broadcasted_iota(jnp.int32, (2 * TILE, TILE), 0) - lax.broadcasted_iota(
        jnp.int32, (2 * TILE, TILE), 1
    )
    band = jnp.where((gap >= AFTER - HW) & (gap <= AFTER + HW), 1.0, 0.0).astype(BF16)
    stride = channels // SRC_DEV
    row = lax.broadcasted_iota(jnp.int32, (16, channels), 0)
    col = lax.broadcasted_iota(jnp.int32, (16, channels), 1)
    pick = jnp.where((col == row * stride) & (row < SRC_DEV), 1.0, 0.0).astype(BF16)
    for t in range(0, FR, TILE):
        total = dot(hi[:, t : t + 2 * TILE], band) + dot(lo[:, t : t + 2 * TILE], band)
        level = total / (2 * HW + 1)
        center = filt_ref[:, AFTER + t : AFTER + t + TILE]
        white = (center / (level + EPS)).astype(BF16)
        for u in range(0, TILE, 128):
            q = (t + u) // 128
            part = white[:, u : u + 128]
            white_ref[channels * q : channels * (q + 1), :] = part
            back = dot(dot(pick, part).astype(BF16), flip).astype(BF16)
            for k in range(SRC_DEV):
                at = k * (FR // 128) + FR // 128 - 1 - q
                src_ref[at : at + 1, :] = back[k : k + 1]


def correlate_kernel(
    half_ref, white_ref, src_ref, out_ref, lhs_ref, nyq_ref, toep0_ref, toep1_ref, acc_ref, *rest, scale
):
    frames = white_ref.shape[0]
    channels = nyq_ref.shape[1]
    count = src_ref.shape[0] // 2
    to_rows = rest[0] if rest else out_ref
    base = half_ref[0] * count
    blocks = FR // TILE
    toeps = (toep0_ref, toep1_ref)
    pad = jnp.zeros((1, TILE), F32)

    def build(s, b):
        to_ref = toeps[s % 2]
        row = src_ref[base + s, b : b + 1, :]

        def store(h, rows):
            at = TILE * b + 16 * h
            to_ref[at : at + 16, :] = rows[:, TILE:]
            to_ref[at + 128 : at + 144, :] = rows[:, TILE - 128 : -128]

        strip(jnp.concatenate([pad, row, pad], 1), 1, store)

    odd = lax.broadcasted_iota(jnp.int32, (channels, 128), 1) % 2 == 1
    for b in range(frames):
        build(0, b)
        total = jnp.zeros((channels, 128), F32)
        for q in range(FR // 128):
            part = white_ref[b, channels * q : channels * (q + 1), :]
            to = channels * (q // 2)
            at = TILE * b + 128 * (q % 2)
            lhs_ref[to : to + channels, at : at + 128] = part
            total += part.astype(F32)
        nyq_ref[b] = jnp.sum(jnp.where(odd, -total, total), axis=1, keepdims=True)

    for s in range(count):
        toep_ref = toeps[s % 2]
        todo = list(range(frames)) if s + 1 < count else []
        for d in (0, 1, -1, 2, -2):
            at = TILE * (2 - d)
            first = channels * max(d, 0)
            rows = channels * (blocks - abs(d))
            res = dot(lhs_ref[first : first + rows, :], toep_ref[:, at : at + TILE])
            to = channels * max(-d, 0)
            if d == 0:
                acc_ref[...] = res
            else:
                acc_ref[to : to + rows, :] += res
            for b in todo[:2]:
                build(s + 1, b)
            todo = todo[2:]

        own = src_ref[base + s]
        lane = lax.broadcasted_iota(jnp.int32, (frames, FR), 1)
        own_nyq = jnp.sum(jnp.where(lane % 2 == 1, own, -own), axis=1, keepdims=True)
        nyq = own_nyq[0:1] * nyq_ref[0]
        for b in range(1, frames):
            nyq += own_nyq[b : b + 1] * nyq_ref[b]
        nyq = jnp.broadcast_to(nyq, (channels, 128))
        nyq = jnp.where(odd, -nyq, nyq) * (scale / (2 * FR))
        nyq = jnp.concatenate([nyq] * (TILE // 128), 1)
        for j in range(blocks):
            part = acc_ref[channels * j : channels * (j + 1), :] * scale - nyq
            for u in range(TILE // 128):
                at = count * (TILE // 128 * j + u) + s
                rows = pl.ds(at, channels, stride=count * (LAGS // 128))
                to_rows[rows, :] = part[:, 128 * u : 128 * (u + 1)]
    if rest:
        out_ref[...] = to_rows[...].astype(out_ref.dtype)


def correlate(half, bundle, src, channels, scale, dtype):
    frames = bundle.shape[0]
    count = src.shape[0] // 2
    shape = (channels * LAGS // 128 * count, 128)
    whole = pl.BlockSpec(memory_space=pltpu.VMEM)
    scratch = [
        pltpu.VMEM((FR // TILE * channels, TILE * frames), BF16),
        pltpu.VMEM((frames, channels, 1), F32),
        pltpu.VMEM((TILE * frames, 5 * TILE), BF16),
        pltpu.VMEM((TILE * frames, 5 * TILE), BF16),
        pltpu.VMEM((FR // TILE * channels, TILE), F32),
    ]
    if dtype != F32:
        scratch.append(pltpu.VMEM(shape, F32))
    return pl.pallas_call(
        functools.partial(correlate_kernel, scale=scale),
        out_shape=jax.ShapeDtypeStruct(shape, dtype),
        in_specs=[pl.BlockSpec(memory_space=pltpu.SMEM), whole, whole],
        out_specs=whole,
        scratch_shapes=scratch,
        compiler_params=pltpu.CompilerParams(vmem_limit_bytes=36 << 20),
    )(half, bundle, src)


def on_device(raw, taps):
    samples, channels = raw.shape
    time_parts = lax.axis_size("tm")
    chan_parts = lax.axis_size("chan")
    chips = time_parts // 2
    place = lax.axis_index("tm")
    core = place % 2
    sources = SRC_DEV * chan_parts // chips
    scale = 1.0 / math.sqrt(samples * time_parts)
    up = [(i, i + 1) for i in range(time_parts - 1)]
    down = [(i + 1, i) for i in range(time_parts - 1)]
    before = lax.ppermute(raw, "tm", up)
    after = lax.ppermute(raw[:AFTER], "tm", down)
    last = (place == time_parts - 1).astype(jnp.int32).reshape(1)
    frame_rows = FR // 128
    whole = pl.BlockSpec(memory_space=pltpu.VMEM)
    white, src = pl.pallas_call(
        whiten_kernel,
        out_shape=(
            jax.ShapeDtypeStruct((frame_rows * channels, 128), BF16),
            jax.ShapeDtypeStruct((SRC_DEV * frame_rows, 128), BF16),
        ),
        grid=(1,),
        in_specs=[
            pl.BlockSpec(memory_space=pltpu.SMEM),
            whole,
            pl.BlockSpec((samples, channels), lambda i: (0, 0)),
            whole,
            pl.BlockSpec((1, TAPS), lambda i: (0, 0)),
        ],
        out_specs=(whole, whole),
        scratch_shapes=[
            pltpu.VMEM((TAPS + TILE, TILE), BF16),
            pltpu.VMEM((channels, BEFORE + FR + AFTER), BF16),
            pltpu.VMEM((channels, FR + 2 * AFTER), F32),
        ],
        compiler_params=pltpu.CompilerParams(vmem_limit_bytes=50 << 20),
    )(last, before, raw, after, taps[None])
    every = lax.all_to_all(
        jnp.broadcast_to(src[None], (chan_parts,) + src.shape), "chan", 0, 0, tiled=True
    )
    every = every.reshape(chips, sources * frame_rows, 128)
    bundle = jnp.concatenate([jnp.broadcast_to(white[None], (chips,) + white.shape), every], 1)
    groups = [[c + 2 * i for i in range(chips)] for c in range(2)]
    bundle = lax.all_to_all(bundle, "tm", 0, 0, tiled=True, axis_index_groups=groups)
    srcs = bundle[:, frame_rows * channels :].astype(F32)
    srcs = srcs.reshape(chips, sources, FR).transpose(1, 0, 2)
    theirs = correlate((1 - core).reshape(1), bundle, srcs, channels, scale, BF16)
    theirs = lax.ppermute(theirs, "tm", [(i, i ^ 1) for i in range(time_parts)])
    ours = correlate(core.reshape(1), bundle, srcs, channels, scale, F32)
    out = ours + theirs.astype(F32)
    out = out.reshape(channels, LAGS // 128, sources // 2, 128).transpose(0, 2, 1, 3)
    return out.reshape(channels, sources // 2, LAGS)


def solution(mesh):
    placed = (P("tm", "chan"), P())
    return jax.shard_map(
        on_device, mesh=mesh, in_specs=placed, out_specs=P("chan", "tm", None), check_vma=False
    )
```

time: 111 us -> 107 us (0.964)
  Pallas kernels: 25.3 us -> 21.4 us
  other arithmetic: 1.56 us -> 3.04 us
    pallas_call x1 -> x0, Pallas kernels: 3.42 us -> none  [finish(): pl.pallas_call(finish_kernel, out_shape=jax.ShapeDtypeStruct((channels *...]
    add x0 -> x1, other arithmetic: none -> 1.49 us  [on_device(): out = ours + theirs.astype(F32)]
  transfers between devices with their start and end apart: 4 -> 4, of which waited for: 1 -> 2; matrix products, arithmetic and copies ran while one was open for 1% -> 1% of each run, Pallas kernels for 9% -> 9%
where the time goes in v2:
time: 107 us
  blocking collectives  32.4 us (30%)
  waiting for transfers between devices  27.7 us (26%)
  Pallas kernels  21.4 us (20%)
  starting transfers between devices  19.4 us (18%)
  other arithmetic  3.04 us (3%)
  local copies, waits for them, and re-layouts  2.92 us (3%)
    all_to_all x1, blocking collectives, on_device(): lax.all_to_all(jnp.broadcast_to(src[None], (chan_parts,) + src.shape), 'c...  32.4 us
    all_to_all x1, waiting for transfers between devices, on_device(): lax.all_to_all(bundle, 'tm', 0, 0, tiled=True, axis_index_groups=groups)  27.5 us
    pallas_call x2, Pallas kernels, correlate(): pl.pallas_call(functools.partial(correlate_kernel, scale=scale), out_shap...  19 us
    ppermute x1, starting transfers between devices, on_device(): after = lax.ppermute(raw[:AFTER], 'tm', down)  5.56 us
    all_to_all x1, starting transfers between devices, on_device(): lax.all_to_all(bundle, 'tm', 0, 0, tiled=True, axis_index_groups=groups)  5.48 us
    ppermute x1, starting transfers between devices, on_device(): before = lax.ppermute(raw, 'tm', up)  4.5 us
    ppermute x1, starting transfers between devices, on_device(): theirs = lax.ppermute(theirs, 'tm', [(i, i ^ 1) for i in range(time_parts)])  3.89 us
    pallas_call x1, Pallas kernels, on_device(): pl.pallas_call(whiten_kernel, out_shape=(jax.ShapeDtypeStruct((frame_rows...  2.41 us
  transfers between devices with their start and end apart: 4, of which 2 were waited for; matrix products, arithmetic and copies ran while one was open for 1% of the time, Pallas kernels for 9%

profile of v2, /device:TPU:1, one launch (start us, length us, event | category | flops | bytes accessed | tf_op | source)
XLA Modules:
  0.0 106.9 jit_solution(11566799591236303211)
XLA Ops:
  0.0 4.5 %collective-permute-start = (bf16[1024,128]{1,0:T(8,128)(2,1)}, bf16[1024,128]{1,0:T(8,128)(2,1)S(1)}, u32[]{:S(2)}, u32[]{:S(2)}) collective-permute-start(bf16[1024,128]{1,0:T(8,128)(2,1)} %raw_ref.1), channel_id=1, source_target_pairs={{0,32},{32,64},{64,96},{96,128},{128,160},{160,192},{192,224},{224... | collective-permute-start | bytes 786440 | tf_op jit(solution)/shard_map/ppermute | solution.py:197
  4.5 0.8 slice.6
  5.3 5.6 %collective-permute-start.1 = (bf16[128,128]{1,0:T(8,128)(2,1)S(1)}, bf16[128,128]{1,0:T(8,128)(2,1)S(1)}, u32[]{:S(2)}, u32[]{:S(2)}) collective-permute-start(bf16[128,128]{1,0:T(8,128)(2,1)S(1)} %slice.6), channel_id=1, source_target_pairs={{32,0},{64,32},{96,64},{128,96},{160,128},{192,160},{224,192},{256... | collective-permute-start | bytes 98312 | tf_op jit(solution)/shard_map/ppermute | solution.py:198
  10.9 0.7 broadcast_in_dim.6.taps_ref
  11.5 0.1 collective-permute-done.1.after_ref
  11.7 0.0 collective-permute-done.before_ref
  11.7 0.0 copy-start
  11.7 0.9 copy-done
  12.6 2.4 %shard_map.28 = (bf16[1024,128]{1,0:T(8,128)(2,1)S(1)}, bf16[16,128]{1,0:T(8,128)(2,1)S(1)}) custom-call(s32[1]{0:T(128)} %bitcast.1.last_ref, bf16[1024,128]{1,0:T(8,128)(2,1)S(1)} %collective-permute-done.before_ref, bf16[1024,128]{1,0:T(8,128)(2,1)S(1)} %copy-done, bf16[128,128]{1,0:T(8,128)(2,1)S(1)} %collective-permute-done.1.after_ref, ...), custom_call_target="tpu_custom_call" | custom-call | tf_op jit(solution)/shard_map/pallas_call | solution.py:202
  15.1 32.4 %all_to_all.10 = bf16[32,16,128]{2,1,0:T(8,128)(2,1)S(1)} all-to-all(bf16[32,16,128]{2,1,0:T(8,128)(2,1)S(1)} %broadcast_in_dim.8), channel_id=1, replica_groups=mesh['tm'=16,'chan'=32] {'chan'}, dimensions={0} | all-to-all | bytes 262144 | tf_op jit(solution)/shard_map/all_to_all | solution.py:224
  47.5 0.3 broadcast_in_dim.7
  47.8 1.5 %pad_maximum_fusion = bf16[8,1088,128]{2,1,0:T(8,128)(2,1)} fusion(bf16[8,64,128]{2,1,0:T(8,128)(2,1)S(1)} %bitcast.14, bf16[8,1024,128]{2,1,0:T(8,128)(2,1)S(1)} %broadcast_in_dim.7), kind=kLoop, calls=%fused_computation | loop fusion | flops 4456448 | bytes 4456448 | tf_op jit(solution)/shard_map/concatenate | solution.py:228
  49.3 5.5 %all-to-all-start.1 = ((bf16[8,1088,128]{2,1,0:T(8,128)(2,1)}), bf16[8,1088,128]{2,1,0:T(8,128)(2,1)S(1)}, u32[]{:S(2)}, u32[]{:S(2)}) async-start(bf16[8,1088,128]{2,1,0:T(8,128)(2,1)} %pad_maximum_fusion), calls=%async_computation.1 | async-start | bytes 4456448 | tf_op jit(solution)/shard_map/all_to_all | solution.py:230
  54.8 27.5 %all-to-all-done.1.white_ref = bf16[8,1088,128]{2,1,0:T(8,128)(2,1)S(1)} async-done(((bf16[8,1088,128]{2,1,0:T(8,128)(2,1)}), bf16[8,1088,128]{2,1,0:T(8,128)(2,1)S(1)}, u32[]{:S(2)}, u32[]{:S(2)}) %all-to-all-start.1) | async-done | bytes 2228256 | tf_op jit(solution)/shard_map/all_to_all | solution.py:230
  82.4 0.2 copy.7
  82.5 9.5 %shard_map.30 = bf16[4096,128]{1,0:T(8,128)(2,1)S(1)} custom-call(s32[1]{0:T(128)} %bitcast.4.half_ref, bf16[8,1088,128]{2,1,0:T(8,128)(2,1)S(1)} %all-to-all-done.1.white_ref, f32[8,8,1024]{2,1,0:T(8,128)S(1)} %bitcast.12), custom_call_target="tpu_custom_call" | custom-call | tf_op jit(solution)/shard_map/pallas_call | solution.py:176
  92.1 3.9 %collective-permute-start.2 = (bf16[4096,128]{1,0:T(8,128)(2,1)S(1)}, bf16[4096,128]{1,0:T(8,128)(2,1)S(1)}, u32[]{:S(2)}, u32[]{:S(2)}) collective-permute-start(bf16[4096,128]{1,0:T(8,128)(2,1)S(1)} %shard_map.30), channel_id=1, source_target_pairs={{0,32},{32,0},{64,96},{96,64},{128,160},{160,128},{192,224},{224,1... | collective-permute-start | bytes 3145736 | tf_op jit(solution)/shard_map/ppermute | solution.py:234
  96.0 9.4 %shard_map.29 = f32[4096,128]{1,0:T(8,128)S(1)} custom-call(s32[1]{0:T(128)} %bitcast.half_ref, bf16[8,1088,128]{2,1,0:T(8,128)(2,1)S(1)} %all-to-all-done.1.white_ref, f32[8,8,1024]{2,1,0:T(8,128)S(1)} %bitcast.13), custom_call_target="tpu_custom_call" | custom-call | tf_op jit(solution)/shard_map/pallas_call | solution.py:176
  105.4 0.0 collective-permute-done.2
  105.4 1.5 %convert_add_fusion = f32[4096,128]{1,0:T(8,128)} fusion(f32[4096,128]{1,0:T(8,128)S(1)} %shard_map.29, bf16[4096,128]{1,0:T(8,128)(2,1)S(1)} %collective-permute-done.2), kind=kLoop, calls=%fused_computation.1 | loop fusion | flops 1048576 | bytes 5242880 | tf_op jit(solution)/shard_map/add | solution.py:236
  (3 shorter events, 0.1 us)
Async XLA Ops:
  0.0 11.7 %collective-permute-start = (bf16[1024,128]{1,0:T(8,128)(2,1)}, bf16[1024,128]{1,0:T(8,128)(2,1)S(1)}, u32[]{:S(2)}, u32[]{:S(2)}) collective-permute-start(bf16[1024,128]{1,0:T(8,128)(2,1)} %raw_ref.1), channel_id=1, source_target_pairs={{0,32},{32,64},{64,96},{96,128},{128,160},{160,192},{192,224},{224... | collective-permute-start | bytes 786440 | tf_op jit(solution)/shard_map/ppermute | solution.py:197
  5.3 6.4 %collective-permute-start.1 = (bf16[128,128]{1,0:T(8,128)(2,1)S(1)}, bf16[128,128]{1,0:T(8,128)(2,1)S(1)}, u32[]{:S(2)}, u32[]{:S(2)}) collective-permute-start(bf16[128,128]{1,0:T(8,128)(2,1)S(1)} %slice.6), channel_id=1, source_target_pairs={{32,0},{64,32},{96,64},{128,96},{160,128},{192,160},{224,192},{256... | collective-permute-start | bytes 98312 | tf_op jit(solution)/shard_map/ppermute | solution.py:198
  11.7 1.0 copy-start
  49.3 33.0 %all-to-all-start.1 = ((bf16[8,1088,128]{2,1,0:T(8,128)(2,1)}), bf16[8,1088,128]{2,1,0:T(8,128)(2,1)S(1)}, u32[]{:S(2)}, u32[]{:S(2)}) async-start(bf16[8,1088,128]{2,1,0:T(8,128)(2,1)} %pad_maximum_fusion), calls=%async_computation.1 | async-start | bytes 4456448 | tf_op jit(solution)/shard_map/all_to_all | solution.py:230
  92.1 13.3 %collective-permute-start.2 = (bf16[4096,128]{1,0:T(8,128)(2,1)S(1)}, bf16[4096,128]{1,0:T(8,128)(2,1)S(1)}, u32[]{:S(2)}, u32[]{:S(2)}) collective-permute-start(bf16[4096,128]{1,0:T(8,128)(2,1)S(1)} %shard_map.30), channel_id=1, source_target_pairs={{0,32},{32,0},{64,96},{96,64},{128,160},{160,128},{192,224},{224,1... | collective-permute-start | bytes 3145736 | tf_op jit(solution)/shard_map/ppermute | solution.py:234

commit v3 on v2

--- a/solution.py
+++ b/solution.py
@@ -88,21 +88,26 @@
                 src_ref[at : at + 1, :] = back[k : k + 1]
 
 
-def correlate_kernel(
-    half_ref, white_ref, src_ref, out_ref, lhs_ref, nyq_ref, toep0_ref, toep1_ref, acc_ref, *rest, scale
-):
-    frames = white_ref.shape[0]
+def correlate_kernel(half_ref, white_ref, src_ref, *refs, scale, count, prior, narrow):
+    refs = list(refs)
+    sources, frames, _ = src_ref.shape
+    group = sources // 2
+    prior_ref = refs.pop(0) if prior else None
+    out_refs = [refs.pop(0) for _ in range(count // group)]
+    lhs_ref, nyq_ref, toep0_ref, toep1_ref, acc_ref = refs[:5]
     channels = nyq_ref.shape[1]
-    count = src_ref.shape[0] // 2
-    to_rows = rest[0] if rest else out_ref
-    base = half_ref[0] * count
+    sum_refs = refs[5:] if narrow else out_refs
+    base = half_ref[0] * group
     blocks = FR // TILE
     toeps = (toep0_ref, toep1_ref)
     pad = jnp.zeros((1, TILE), F32)
 
+    def place(s):
+        return lax.rem(base + s, sources)
+
     def build(s, b):
         to_ref = toeps[s % 2]
-        row = src_ref[base + s, b : b + 1, :]
+        row = src_ref[place(s), b : b + 1, :]
 
         def store(h, rows):
             at = TILE * b + 16 * h
@@ -136,11 +141,11 @@
                 acc_ref[...] = res
             else:
                 acc_ref[to : to + rows, :] += res
-            for b in todo[:2]:
+            for b in todo[:1]:
                 build(s + 1, b)
-            todo = todo[2:]
-
-        own = src_ref[base + s]
+            todo = todo[1:]
+
+        own = src_ref[place(s)]
         lane = lax.broadcasted_iota(jnp.int32, (frames, FR), 1)
         own_nyq = jnp.sum(jnp.where(lane % 2 == 1, own, -own), axis=1, keepdims=True)
         nyq = own_nyq[0:1] * nyq_ref[0]
@@ -148,22 +153,28 @@
             nyq += own_nyq[b : b + 1] * nyq_ref[b]
         nyq = jnp.broadcast_to(nyq, (channels, 128))
         nyq = jnp.where(odd, -nyq, nyq) * (scale / (2 * FR))
-        nyq = jnp.concatenate([nyq] * (TILE // 128), 1)
-        for j in range(blocks):
-            part = acc_ref[channels * j : channels * (j + 1), :] * scale - nyq
-            for u in range(TILE // 128):
-                at = count * (TILE // 128 * j + u) + s
-                rows = pl.ds(at, channels, stride=count * (LAGS // 128))
-                to_rows[rows, :] = part[:, 128 * u : 128 * (u + 1)]
-    if rest:
-        out_ref[...] = to_rows[...].astype(out_ref.dtype)
-
-
-def correlate(half, bundle, src, channels, scale, dtype):
+        for q in range(LAGS // 128):
+            j, u = divmod(q, TILE // 128)
+            lanes = slice(128 * u, 128 * (u + 1))
+            part = acc_ref[channels * j : channels * (j + 1), lanes] * scale - nyq
+            at = channels * (blocks * (s % group) + j)
+            plain = slice(at, at + channels)
+            if prior:
+                rows = pl.ds(group * q + s, channels, stride=group * (LAGS // 128))
+                sum_refs[0][rows, :] = part + prior_ref[plain, lanes]
+            else:
+                sum_refs[s // group][plain, lanes] = part
+    if narrow:
+        out_refs[0][...] = sum_refs[0][...].astype(BF16)
+
+
+def correlate(half, bundle, src, channels, scale, count, prior=None, narrow=False):
     frames = bundle.shape[0]
-    count = src.shape[0] // 2
-    shape = (channels * LAGS // 128 * count, 128)
+    group = src.shape[0] // 2
+    block = TILE if prior is None else 128
+    shape = (channels * (LAGS // block) * group, block)
     whole = pl.BlockSpec(memory_space=pltpu.VMEM)
+    extra = [] if prior is None else [prior]
     scratch = [
         pltpu.VMEM((FR // TILE * channels, TILE * frames), BF16),
         pltpu.VMEM((frames, channels, 1), F32),
@@ -171,16 +182,19 @@
         pltpu.VMEM((TILE * frames, 5 * TILE), BF16),
         pltpu.VMEM((FR // TILE * channels, TILE), F32),
     ]
-    if dtype != F32:
+    if narrow:
         scratch.append(pltpu.VMEM(shape, F32))
+    outs = count // group
     return pl.pallas_call(
-        functools.partial(correlate_kernel, scale=scale),
-        out_shape=jax.ShapeDtypeStruct(shape, dtype),
-        in_specs=[pl.BlockSpec(memory_space=pltpu.SMEM), whole, whole],
-        out_specs=whole,
+        functools.partial(
+            correlate_kernel, scale=scale, count=count, prior=prior is not None, narrow=narrow
+        ),
+        out_shape=[jax.ShapeDtypeStruct(shape, BF16 if narrow else F32)] * outs,
+        in_specs=[pl.BlockSpec(memory_space=pltpu.SMEM)] + [whole] * (2 + len(extra)),
+        out_specs=[whole] * outs,
         scratch_shapes=scratch,
-        compiler_params=pltpu.CompilerParams(vmem_limit_bytes=36 << 20),
-    )(half, bundle, src)
+        compiler_params=pltpu.CompilerParams(vmem_limit_bytes=28 << 20),
+    )(half, bundle, src, *extra)
 
 
 def on_device(raw, taps):
@@ -224,18 +238,39 @@
     every = lax.all_to_all(
         jnp.broadcast_to(src[None], (chan_parts,) + src.shape), "chan", 0, 0, tiled=True
     )
-    every = every.reshape(chips, sources * frame_rows, 128)
-    bundle = jnp.concatenate([jnp.broadcast_to(white[None], (chips,) + white.shape), every], 1)
-    groups = [[c + 2 * i for i in range(chips)] for c in range(2)]
-    bundle = lax.all_to_all(bundle, "tm", 0, 0, tiled=True, axis_index_groups=groups)
-    srcs = bundle[:, frame_rows * channels :].astype(F32)
-    srcs = srcs.reshape(chips, sources, FR).transpose(1, 0, 2)
-    theirs = correlate((1 - core).reshape(1), bundle, srcs, channels, scale, BF16)
+    lines = chips // 2
+    place = lax.optimization_barrier((place, every[0, 0, 0]))[0]
+    core = place % 2
+    side = place // 2 % 2
+    every = every.reshape(lines, 2, sources * frame_rows, 128)
+    mine = lax.dynamic_index_in_dim(every, side, 1, keepdims=False)
+    others = lax.dynamic_index_in_dim(every, 1 - side, 1, keepdims=False)
+    far = jnp.concatenate([white, others.reshape(-1, 128)], 0)
+    far = lax.ppermute(far, "tm", [(i, i ^ 2) for i in range(time_parts)])
+    groups = [[c + 4 * i for i in range(lines)] for c in range(4)]
+
+    def gather(frame, srcs):
+        both = jnp.concatenate([jnp.broadcast_to(frame[None], (lines,) + frame.shape), srcs], 1)
+        return lax.all_to_all(both, "tm", 0, 0, tiled=True, axis_index_groups=groups)
+
+    def signals(bundle):
+        srcs = bundle[:, frame_rows * channels :].astype(F32)
+        return srcs.reshape(lines, sources, FR).transpose(1, 0, 2)
+
+    near = gather(white, mine)
+    far = lax.optimization_barrier((far, near[0, 0, 0]))[0]
+    far = gather(far[: white.shape[0]], far[white.shape[0] :].reshape(mine.shape))
+    other = (1 - core).reshape(1)
+    own = core.reshape(1)
+    parts = correlate(other, near, signals(near), channels, scale, sources)
+    half = sources // 2
+    srcs = signals(far)
+    theirs = correlate(other, far, srcs, channels, scale, half, parts[0], True)[0]
     theirs = lax.ppermute(theirs, "tm", [(i, i ^ 1) for i in range(time_parts)])
-    ours = correlate(core.reshape(1), bundle, srcs, channels, scale, F32)
+    ours = correlate(own, far, srcs, channels, scale, half, parts[1])[0]
     out = ours + theirs.astype(F32)
-    out = out.reshape(channels, LAGS // 128, sources // 2, 128).transpose(0, 2, 1, 3)
-    return out.reshape(channels, sources // 2, LAGS)
+    out = out.reshape(channels, LAGS // 128, half, 128).transpose(0, 2, 1, 3)
+    return out.reshape(channels, half, LAGS)
 
 
 def solution(mesh):

time: 107 us -> 106 us (level)
  the two profiles are of different devices: /device:TPU:1 before, /device:TPU:7 now
where the time goes in v3:
time: 106 us; the launch traced here: 105 us
  starting transfers between devices  36.1 us (34%)
  waiting for transfers between devices  35 us (33%)
  Pallas kernels  22.3 us (21%)
  local copies, waits for them, and re-layouts  7.88 us (7%)
  other arithmetic  3.74 us (4%)
    pallas_call x3, Pallas kernels, correlate(): pl.pallas_call(functools.partial(correlate_kernel, scale=scale, count=cou...  19.9 us
    all_to_all x1, starting transfers between devices, on_device(): lax.all_to_all(jnp.broadcast_to(src[None], (chan_parts,) + src.shape), 'c...  17.6 us
    all_to_all x1, waiting for transfers between devices, on_device(): lax.all_to_all(jnp.broadcast_to(src[None], (chan_parts,) + src.shape), 'c...  14.9 us
    ppermute x1, waiting for transfers between devices, on_device(): far = lax.ppermute(far, 'tm', [(i, i ^ 2) for i in range(time_parts)])  9.37 us
    all_to_all x2, starting transfers between devices, gather(): lax.all_to_all(both, 'tm', 0, 0, tiled=True, axis_index_groups=groups)  7.88 us
    all_to_all x2, waiting for transfers between devices, gather(): lax.all_to_all(both, 'tm', 0, 0, tiled=True, axis_index_groups=groups)  7.22 us
    unnamed x10, local copies, waits for them, and re-layouts  5.19 us
    ppermute x1, starting transfers between devices, on_device(): before = lax.ppermute(raw, 'tm', up)  4.02 us
  transfers between devices with their start and end apart: 7, of which 5 were waited for; matrix products, arithmetic and copies ran while one was open for 3% of the time, Pallas kernels for 13%

profile of v3, /device:TPU:7, one launch (start us, length us, event | category | flops | bytes accessed | tf_op | source)
XLA Modules:
  0.0 105.3 jit_solution(13652100898653557315)
XLA Ops:
  0.0 4.0 %collective-permute-start = (bf16[1024,128]{1,0:T(8,128)(2,1)}, bf16[1024,128]{1,0:T(8,128)(2,1)S(1)}, u32[]{:S(2)}, u32[]{:S(2)}) collective-permute-start(bf16[1024,128]{1,0:T(8,128)(2,1)} %raw_ref.1), channel_id=1, source_target_pairs={{0,32},{32,64},{64,96},{96,128},{128,160},{160,192},{192,224},{224... | collective-permute-start | bytes 786440 | tf_op jit(solution)/shard_map/ppermute | solution.py:211
  4.0 0.8 slice.17
  4.8 1.9 %collective-permute-start.1 = (bf16[128,128]{1,0:T(8,128)(2,1)S(1)}, bf16[128,128]{1,0:T(8,128)(2,1)S(1)}, u32[]{:S(2)}, u32[]{:S(2)}) collective-permute-start(bf16[128,128]{1,0:T(8,128)(2,1)S(1)} %slice.17), channel_id=1, source_target_pairs={{32,0},{64,32},{96,64},{128,96},{160,128},{192,160},{224,192},{256... | collective-permute-start | bytes 98312 | tf_op jit(solution)/shard_map/ppermute | solution.py:212
  6.7 0.7 broadcast_in_dim.8.taps_ref
  7.4 3.5 %collective-permute-done.1.after_ref = bf16[128,128]{1,0:T(8,128)(2,1)S(1)} collective-permute-done((bf16[128,128]{1,0:T(8,128)(2,1)S(1)}, bf16[128,128]{1,0:T(8,128)(2,1)S(1)}, u32[]{:S(2)}, u32[]{:S(2)}) %collective-permute-start.1) | collective-permute-done | bytes 32800 | tf_op jit(solution)/shard_map/ppermute | solution.py:212
  10.9 0.9 copy-done.4
  11.9 2.4 %shard_map.28 = (bf16[1024,128]{1,0:T(8,128)(2,1)S(1)}, bf16[16,128]{1,0:T(8,128)(2,1)S(1)}) custom-call(s32[1]{0:T(128)} %bitcast.1.last_ref, bf16[1024,128]{1,0:T(8,128)(2,1)S(1)} %collective-permute-done.before_ref, bf16[1024,128]{1,0:T(8,128)(2,1)S(1)} %copy-done.4, bf16[128,128]{1,0:T(8,128)(2,1)S(1)} %collective-permute-done.1.after_ref, ...), custom_call_target="tpu_custom_call" | custom-call | tf_op jit(solution)/shard_map/pallas_call | solution.py:216
  14.3 0.7 broadcast_in_dim.9
  15.0 17.6 %all-to-all-start = ((bf16[32,16,128]{2,1,0:T(8,128)(2,1)}), bf16[32,16,128]{2,1,0:T(8,128)(2,1)S(1)}, u32[]{:S(2)}, u32[]{:S(2)}) async-start(bf16[32,16,128]{2,1,0:T(8,128)(2,1)} %broadcast_in_dim.9), calls=%async_computation | async-start | bytes 262144 | tf_op jit(solution)/shard_map/all_to_all | solution.py:238
  32.7 14.9 %all-to-all-done = bf16[32,16,128]{2,1,0:T(8,128)(2,1)S(1)} async-done(((bf16[32,16,128]{2,1,0:T(8,128)(2,1)}), bf16[32,16,128]{2,1,0:T(8,128)(2,1)S(1)}, u32[]{:S(2)}, u32[]{:S(2)}) %all-to-all-start) | async-done | bytes 131104 | tf_op jit(solution)/shard_map/all_to_all | solution.py:238
  47.6 0.1 broadcast_in_dim.11
  47.7 1.1 %pad_maximum_fusion.1 = bf16[4,1088,128]{2,1,0:T(8,128)(2,1)} fusion(bf16[4,64,128]{2,1,0:T(8,128)(2,1)S(1)} %get-tuple-element.13, bf16[4,1024,128]{2,1,0:T(8,128)(2,1)S(1)} %broadcast_in_dim.11), kind=kLoop, calls=%fused_computation.2 | loop fusion | flops 2228224 | bytes 2228224 | tf_op jit(solution)/shard_map/concatenate | solution.py:253
  48.8 4.2 %all-to-all-start.2 = ((bf16[4,1088,128]{2,1,0:T(8,128)(2,1)}), bf16[4,1088,128]{2,1,0:T(8,128)(2,1)S(1)}, u32[]{:S(2)}, u32[]{:S(2)}) async-start(bf16[4,1088,128]{2,1,0:T(8,128)(2,1)} %pad_maximum_fusion.1), calls=%async_computation.2 | async-start | bytes 2228224 | tf_op jit(solution)/shard_map/all_to_all | solution.py:254
  53.0 1.9 %collective-permute-start.2 = (bf16[1280,128]{1,0:T(8,128)(2,1)S(1)}, bf16[1280,128]{1,0:T(8,128)(2,1)S(1)}, u32[]{:S(2)}, u32[]{:S(2)}) collective-permute-start(bf16[1280,128]{1,0:T(8,128)(2,1)S(1)} %pad_maximum_fusion.2), channel_id=1, source_target_pairs={{0,64},{32,96},{64,0},{96,32},{128,192},{160,224},{192,128},{224,1... | collective-permute-start | bytes 983048 | tf_op jit(solution)/shard_map/ppermute | solution.py:249
  54.9 9.4 %collective-permute-done.2 = bf16[1280,128]{1,0:T(8,128)(2,1)S(1)} collective-permute-done((bf16[1280,128]{1,0:T(8,128)(2,1)S(1)}, bf16[1280,128]{1,0:T(8,128)(2,1)S(1)}, u32[]{:S(2)}, u32[]{:S(2)}) %collective-permute-start.2) | collective-permute-done | bytes 327712 | tf_op jit(solution)/shard_map/ppermute | solution.py:249
  64.3 0.1 broadcast_in_dim.10
  64.5 1.1 %pad_maximum_fusion = bf16[4,1088,128]{2,1,0:T(8,128)(2,1)} fusion(bf16[4,64,128]{2,1,0:T(8,128)(2,1)S(1)} %bitcast.23, bf16[4,1024,128]{2,1,0:T(8,128)(2,1)S(1)} %broadcast_in_dim.10), kind=kLoop, calls=%fused_computation.1 | loop fusion | flops 2228224 | bytes 2228224 | tf_op jit(solution)/shard_map/concatenate | solution.py:253
  65.5 2.8 %all-to-all-done.2.white_ref = bf16[4,1088,128]{2,1,0:T(8,128)(2,1)S(1)} async-done(((bf16[4,1088,128]{2,1,0:T(8,128)(2,1)}), bf16[4,1088,128]{2,1,0:T(8,128)(2,1)S(1)}, u32[]{:S(2)}, u32[]{:S(2)}) %all-to-all-start.2) | async-done | bytes 1114144 | tf_op jit(solution)/shard_map/all_to_all | solution.py:254
  68.3 3.7 %all-to-all-start.1 = ((bf16[4,1088,128]{2,1,0:T(8,128)(2,1)}), bf16[4,1088,128]{2,1,0:T(8,128)(2,1)S(1)}, u32[]{:S(2)}, u32[]{:S(2)}) async-start(bf16[4,1088,128]{2,1,0:T(8,128)(2,1)} %pad_maximum_fusion), calls=%async_computation.1 | async-start | bytes 2228224 | tf_op jit(solution)/shard_map/all_to_all | solution.py:254
  72.1 0.1 copy.9
  72.2 8.5 %shard_map.29 = (f32[2048,256]{1,0:T(8,128)S(1)}, f32[2048,256]{1,0:T(8,128)S(1)}) custom-call(s32[1]{0:T(128)} %bitcast.6.half_ref, bf16[4,1088,128]{2,1,0:T(8,128)(2,1)S(1)} %all-to-all-done.2.white_ref, f32[8,4,1024]{2,1,0:T(4,128)S(1)} %bitcast.21), custom_call_target="tpu_custom_call" | custom-call | tf_op jit(solution)/shard_map/pallas_call | solution.py:188
  80.7 0.0 copy-start
  80.7 1.3 %copy-done = f32[2048,256]{1,0:T(8,128)} copy-done((f32[2048,256]{1,0:T(8,128)}, f32[2048,256]{1,0:T(8,128)S(1)}, u32[]{:S(2)}) %copy-start) | copy-done | bytes 2097176
  82.0 1.3 %copy-done.2 = f32[2048,256]{1,0:T(8,128)} copy-done((f32[2048,256]{1,0:T(8,128)}, f32[2048,256]{1,0:T(8,128)S(1)}, u32[]{:S(2)}) %copy-start.2) | copy-done | bytes 2097176
  83.3 4.4 %all-to-all-done.1.white_ref = bf16[4,1088,128]{2,1,0:T(8,128)(2,1)S(1)} async-done(((bf16[4,1088,128]{2,1,0:T(8,128)(2,1)}), bf16[4,1088,128]{2,1,0:T(8,128)(2,1)S(1)}, u32[]{:S(2)}, u32[]{:S(2)}) %all-to-all-start.1) | async-done | bytes 1114144 | tf_op jit(solution)/shard_map/all_to_all | solution.py:254
  87.8 0.1 copy.10
  87.9 1.6 %copy-done.3 = f32[2048,256]{1,0:T(8,128)S(1)} copy-done((f32[2048,256]{1,0:T(8,128)S(1)}, f32[2048,256]{1,0:T(8,128)}, u32[]{:S(2)}) %copy-start.3) | copy-done | bytes 2097176
  89.5 5.9 %shard_map.31 = bf16[4096,128]{1,0:T(8,128)(2,1)S(1)} custom-call(s32[1]{0:T(128)} %bitcast.6.half_ref, bf16[4,1088,128]{2,1,0:T(8,128)(2,1)S(1)} %all-to-all-done.1.white_ref, f32[8,4,1024]{2,1,0:T(4,128)S(1)} %bitcast.19, f32[2048,256]{1,0:T(8,128)S(1)} %copy-done.3), custom_call_target="tpu_custom_call" | custom-call | tf_op jit(solution)/shard_map/pallas_call | solution.py:188
  95.4 2.8 %collective-permute-start.3 = (bf16[4096,128]{1,0:T(8,128)(2,1)S(1)}, bf16[4096,128]{1,0:T(8,128)(2,1)S(1)}, u32[]{:S(2)}, u32[]{:S(2)}) collective-permute-start(bf16[4096,128]{1,0:T(8,128)(2,1)S(1)} %shard_map.31), channel_id=1, source_target_pairs={{0,32},{32,0},{64,96},{96,64},{128,160},{160,128},{192,224},{224,1... | collective-permute-start | bytes 3145736 | tf_op jit(solution)/shard_map/ppermute | solution.py:269
  98.2 5.6 %shard_map.30 = f32[4096,128]{1,0:T(8,128)S(1)} custom-call(s32[1]{0:T(128)} %bitcast.half_ref, bf16[4,1088,128]{2,1,0:T(8,128)(2,1)S(1)} %all-to-all-done.1.white_ref, f32[8,4,1024]{2,1,0:T(4,128)S(1)} %bitcast.20, f32[2048,256]{1,0:T(8,128)S(1)} %copy-done.1), custom_call_target="tpu_custom_call" | custom-call | tf_op jit(solution)/shard_map/pallas_call | solution.py:188
  103.7 0.0 collective-permute-done.3
  103.7 1.6 %convert_add_fusion = f32[4096,128]{1,0:T(8,128)} fusion(f32[4096,128]{1,0:T(8,128)S(1)} %shard_map.30, bf16[4096,128]{1,0:T(8,128)(2,1)S(1)} %collective-permute-done.3), kind=kLoop, calls=%fused_computation | loop fusion | flops 1048576 | bytes 5242880 | tf_op jit(solution)/shard_map/add | solution.py:271
  (14 shorter events, 0.1 us)
Async XLA Ops:
  0.0 10.9 %collective-permute-start = (bf16[1024,128]{1,0:T(8,128)(2,1)}, bf16[1024,128]{1,0:T(8,128)(2,1)S(1)}, u32[]{:S(2)}, u32[]{:S(2)}) collective-permute-start(bf16[1024,128]{1,0:T(8,128)(2,1)} %raw_ref.1), channel_id=1, source_target_pairs={{0,32},{32,64},{64,96},{96,128},{128,160},{160,192},{192,224},{224... | collective-permute-start | bytes 786440 | tf_op jit(solution)/shard_map/ppermute | solution.py:211
  4.8 6.1 %collective-permute-start.1 = (bf16[128,128]{1,0:T(8,128)(2,1)S(1)}, bf16[128,128]{1,0:T(8,128)(2,1)S(1)}, u32[]{:S(2)}, u32[]{:S(2)}) collective-permute-start(bf16[128,128]{1,0:T(8,128)(2,1)S(1)} %slice.17), channel_id=1, source_target_pairs={{32,0},{64,32},{96,64},{128,96},{160,128},{192,160},{224,192},{256... | collective-permute-start | bytes 98312 | tf_op jit(solution)/shard_map/ppermute | solution.py:212
  10.9 1.0 copy-start.4
  15.0 32.6 %all-to-all-start = ((bf16[32,16,128]{2,1,0:T(8,128)(2,1)}), bf16[32,16,128]{2,1,0:T(8,128)(2,1)S(1)}, u32[]{:S(2)}, u32[]{:S(2)}) async-start(bf16[32,16,128]{2,1,0:T(8,128)(2,1)} %broadcast_in_dim.9), calls=%async_computation | async-start | bytes 262144 | tf_op jit(solution)/shard_map/all_to_all | solution.py:238
  48.8 19.6 %all-to-all-start.2 = ((bf16[4,1088,128]{2,1,0:T(8,128)(2,1)}), bf16[4,1088,128]{2,1,0:T(8,128)(2,1)S(1)}, u32[]{:S(2)}, u32[]{:S(2)}) async-start(bf16[4,1088,128]{2,1,0:T(8,128)(2,1)} %pad_maximum_fusion.1), calls=%async_computation.2 | async-start | bytes 2228224 | tf_op jit(solution)/shard_map/all_to_all | solution.py:254
  53.0 11.3 %collective-permute-start.2 = (bf16[1280,128]{1,0:T(8,128)(2,1)S(1)}, bf16[1280,128]{1,0:T(8,128)(2,1)S(1)}, u32[]{:S(2)}, u32[]{:S(2)}) collective-permute-start(bf16[1280,128]{1,0:T(8,128)(2,1)S(1)} %pad_maximum_fusion.2), channel_id=1, source_target_pairs={{0,64},{32,96},{64,0},{96,32},{128,192},{160,224},{192,128},{224,1... | collective-permute-start | bytes 983048 | tf_op jit(solution)/shard_map/ppermute | solution.py:249
  68.3 19.4 %all-to-all-start.1 = ((bf16[4,1088,128]{2,1,0:T(8,128)(2,1)}), bf16[4,1088,128]{2,1,0:T(8,128)(2,1)S(1)}, u32[]{:S(2)}, u32[]{:S(2)}) async-start(bf16[4,1088,128]{2,1,0:T(8,128)(2,1)} %pad_maximum_fusion), calls=%async_computation.1 | async-start | bytes 2228224 | tf_op jit(solution)/shard_map/all_to_all | solution.py:254
  80.7 1.3 %copy-start = (f32[2048,256]{1,0:T(8,128)}, f32[2048,256]{1,0:T(8,128)S(1)}, u32[]{:S(2)}) copy-start(f32[2048,256]{1,0:T(8,128)S(1)} %get-tuple-element.11.refs_0_) | copy-start | bytes 6291460
  82.0 1.3 %copy-start.2 = (f32[2048,256]{1,0:T(8,128)}, f32[2048,256]{1,0:T(8,128)S(1)}, u32[]{:S(2)}) copy-start(f32[2048,256]{1,0:T(8,128)S(1)} %get-tuple-element.12.refs_0_) | copy-start | bytes 6291460
  87.9 1.6 %copy-start.3 = (f32[2048,256]{1,0:T(8,128)S(1)}, f32[2048,256]{1,0:T(8,128)}, u32[]{:S(2)}) copy-start(f32[2048,256]{1,0:T(8,128)} %copy-done.2) | copy-start | bytes 6291460
  89.5 8.7 %copy-start.1 = (f32[2048,256]{1,0:T(8,128)S(1)}, f32[2048,256]{1,0:T(8,128)}, u32[]{:S(2)}) copy-start(f32[2048,256]{1,0:T(8,128)} %copy-done) | copy-start | bytes 6291460
  95.4 8.3 %collective-permute-start.3 = (bf16[4096,128]{1,0:T(8,128)(2,1)S(1)}, bf16[4096,128]{1,0:T(8,128)(2,1)S(1)}, u32[]{:S(2)}, u32[]{:S(2)}) collective-permute-start(bf16[4096,128]{1,0:T(8,128)(2,1)S(1)} %shard_map.31), channel_id=1, source_target_pairs={{0,32},{32,0},{64,96},{96,64},{128,160},{160,128},{192,224},{224,1... | collective-permute-start | bytes 3145736 | tf_op jit(solution)/shard_map/ppermute | solution.py:269

commit v4 on v3

--- a/solution.py
+++ b/solution.py
@@ -90,7 +90,9 @@
 
 def correlate_kernel(half_ref, white_ref, src_ref, *refs, scale, count, prior, narrow):
     refs = list(refs)
-    sources, frames, _ = src_ref.shape
+    frames, src_rows, _ = src_ref.shape
+    frame_rows = FR // 128
+    sources = src_rows // frame_rows
     group = sources // 2
     prior_ref = refs.pop(0) if prior else None
     out_refs = [refs.pop(0) for _ in range(count // group)]
@@ -102,12 +104,14 @@
     toeps = (toep0_ref, toep1_ref)
     pad = jnp.zeros((1, TILE), F32)
 
-    def place(s):
-        return lax.rem(base + s, sources)
+    def signal(s, b):
+        at = pl.multiple_of(lax.rem(base + s, sources) * frame_rows, frame_rows)
+        return src_ref[b, pl.ds(at, frame_rows), :]
 
     def build(s, b):
         to_ref = toeps[s % 2]
-        row = src_ref[place(s), b : b + 1, :]
+        rows = signal(s, b)
+        row = jnp.concatenate([rows[q : q + 1] for q in range(frame_rows)], 1)
 
         def store(h, rows):
             at = TILE * b + 16 * h
@@ -145,12 +149,11 @@
                 build(s + 1, b)
             todo = todo[1:]
 
-        own = src_ref[place(s)]
-        lane = lax.broadcasted_iota(jnp.int32, (frames, FR), 1)
-        own_nyq = jnp.sum(jnp.where(lane % 2 == 1, own, -own), axis=1, keepdims=True)
-        nyq = own_nyq[0:1] * nyq_ref[0]
-        for b in range(1, frames):
-            nyq += own_nyq[b : b + 1] * nyq_ref[b]
+        nyq = jnp.zeros((channels, 1), F32)
+        for b in range(frames):
+            own = signal(s, b)
+            own = jnp.sum(jnp.where(odd[:frame_rows], own, -own), axis=1, keepdims=True)
+            nyq += jnp.sum(own, axis=0, keepdims=True) * nyq_ref[b]
         nyq = jnp.broadcast_to(nyq, (channels, 128))
         nyq = jnp.where(odd, -nyq, nyq) * (scale / (2 * FR))
         for q in range(LAGS // 128):
@@ -161,16 +164,16 @@
             plain = slice(at, at + channels)
             if prior:
                 rows = pl.ds(group * q + s, channels, stride=group * (LAGS // 128))
-                sum_refs[0][rows, :] = part + prior_ref[plain, lanes]
+                sum_refs[0][rows, :] = part + prior_ref[plain, lanes].astype(F32)
             else:
-                sum_refs[s // group][plain, lanes] = part
+                sum_refs[s // group][plain, lanes] = part.astype(sum_refs[0].dtype)
     if narrow:
         out_refs[0][...] = sum_refs[0][...].astype(BF16)
 
 
 def correlate(half, bundle, src, channels, scale, count, prior=None, narrow=False):
     frames = bundle.shape[0]
-    group = src.shape[0] // 2
+    group = src.shape[1] // (FR // 128) // 2
     block = TILE if prior is None else 128
     shape = (channels * (LAGS // block) * group, block)
     whole = pl.BlockSpec(memory_space=pltpu.VMEM)
@@ -189,7 +192,7 @@
         functools.partial(
             correlate_kernel, scale=scale, count=count, prior=prior is not None, narrow=narrow
         ),
-        out_shape=[jax.ShapeDtypeStruct(shape, BF16 if narrow else F32)] * outs,
+        out_shape=[jax.ShapeDtypeStruct(shape, BF16 if narrow or prior is None else F32)] * outs,
         in_specs=[pl.BlockSpec(memory_space=pltpu.SMEM)] + [whole] * (2 + len(extra)),
         out_specs=[whole] * outs,
         scratch_shapes=scratch,
@@ -239,7 +242,7 @@
         jnp.broadcast_to(src[None], (chan_parts,) + src.shape), "chan", 0, 0, tiled=True
     )
     lines = chips // 2
-    place = lax.optimization_barrier((place, every[0, 0, 0]))[0]
+    place, white, _ = lax.optimization_barrier((place, white, every[0, 0, 0]))
     core = place % 2
     side = place // 2 % 2
     every = every.reshape(lines, 2, sources * frame_rows, 128)
@@ -254,8 +257,7 @@
         return lax.all_to_all(both, "tm", 0, 0, tiled=True, axis_index_groups=groups)
 
     def signals(bundle):
-        srcs = bundle[:, frame_rows * channels :].astype(F32)
-        return srcs.reshape(lines, sources, FR).transpose(1, 0, 2)
+        return bundle[:, frame_rows * channels :].astype(F32)
 
     near = gather(white, mine)
     far = lax.optimization_barrier((far, near[0, 0, 0]))[0]

time: 106 us -> 105 us (level)
  local copies, waits for them, and re-layouts: 7.88 us -> 5.6 us
  waiting for transfers between devices: 35 us -> 36.7 us
    unnamed x10 -> x6, local copies, waits for them, and re-layouts: 5.19 us -> 3.14 us
    all_to_all x2, waiting for transfers between devices: 7.22 us -> 8.92 us  [gather(): lax.all_to_all(both, 'tm', 0, 0, tiled=True, axis_index_groups=groups)]
where the time goes in v4:
time: 105 us
  waiting for transfers between devices  36.7 us (35%)
  starting transfers between devices  36.1 us (34%)
  Pallas kernels  22.4 us (21%)
  local copies, waits for them, and re-layouts  5.6 us (5%)
  other arithmetic  3.74 us (4%)
    pallas_call x3, Pallas kernels, correlate(): pl.pallas_call(functools.partial(correlate_kernel, scale=scale, count=cou...  20 us
    all_to_all x1, starting transfers between devices, on_device(): lax.all_to_all(jnp.broadcast_to(src[None], (chan_parts,) + src.shape), 'c...  17.6 us
    all_to_all x1, waiting for transfers between devices, on_device(): lax.all_to_all(jnp.broadcast_to(src[None], (chan_parts,) + src.shape), 'c...  14.9 us
    ppermute x1, waiting for transfers between devices, on_device(): far = lax.ppermute(far, 'tm', [(i, i ^ 2) for i in range(time_parts)])  9.37 us
    all_to_all x2, waiting for transfers between devices, gather(): lax.all_to_all(both, 'tm', 0, 0, tiled=True, axis_index_groups=groups)  8.92 us
    all_to_all x2, starting transfers between devices, gather(): lax.all_to_all(both, 'tm', 0, 0, tiled=True, axis_index_groups=groups)  7.88 us
    ppermute x1, starting transfers between devices, on_device(): before = lax.ppermute(raw, 'tm', up)  4.02 us
    ppermute x1, waiting for transfers between devices, on_device(): after = lax.ppermute(raw[:AFTER], 'tm', down)  3.51 us
  transfers between devices with their start and end apart: 7, of which 5 were waited for; matrix products, arithmetic and copies ran while one was open for 3% of the time, Pallas kernels for 13%

profile of v4, /device:TPU:7, one launch (start us, length us, event | category | flops | bytes accessed | tf_op | source)
XLA Modules:
  0.0 104.8 jit_solution(16296587246177389576)
XLA Ops:
  0.0 4.0 %collective-permute-start = (bf16[1024,128]{1,0:T(8,128)(2,1)}, bf16[1024,128]{1,0:T(8,128)(2,1)S(1)}, u32[]{:S(2)}, u32[]{:S(2)}) collective-permute-start(bf16[1024,128]{1,0:T(8,128)(2,1)} %raw_ref.1), channel_id=1, source_target_pairs={{0,32},{32,64},{64,96},{96,128},{128,160},{160,192},{192,224},{224... | collective-permute-start | bytes 786440 | tf_op jit(solution)/shard_map/ppermute | solution.py:214
  4.0 0.8 slice.17
  4.8 1.9 %collective-permute-start.1 = (bf16[128,128]{1,0:T(8,128)(2,1)S(1)}, bf16[128,128]{1,0:T(8,128)(2,1)S(1)}, u32[]{:S(2)}, u32[]{:S(2)}) collective-permute-start(bf16[128,128]{1,0:T(8,128)(2,1)S(1)} %slice.17), channel_id=1, source_target_pairs={{32,0},{64,32},{96,64},{128,96},{160,128},{192,160},{224,192},{256... | collective-permute-start | bytes 98312 | tf_op jit(solution)/shard_map/ppermute | solution.py:215
  6.7 0.7 broadcast_in_dim.8.taps_ref
  7.4 3.5 %collective-permute-done.1.after_ref = bf16[128,128]{1,0:T(8,128)(2,1)S(1)} collective-permute-done((bf16[128,128]{1,0:T(8,128)(2,1)S(1)}, bf16[128,128]{1,0:T(8,128)(2,1)S(1)}, u32[]{:S(2)}, u32[]{:S(2)}) %collective-permute-start.1) | collective-permute-done | bytes 32800 | tf_op jit(solution)/shard_map/ppermute | solution.py:215
  10.9 0.0 collective-permute-done.before_ref
  10.9 0.0 copy-start.2
  10.9 0.9 copy-done.2
  11.9 2.4 %shard_map.28 = (bf16[1024,128]{1,0:T(8,128)(2,1)S(1)}, bf16[16,128]{1,0:T(8,128)(2,1)S(1)}) custom-call(s32[1]{0:T(128)} %bitcast.last_ref, bf16[1024,128]{1,0:T(8,128)(2,1)S(1)} %collective-permute-done.before_ref, bf16[1024,128]{1,0:T(8,128)(2,1)S(1)} %copy-done.2, bf16[128,128]{1,0:T(8,128)(2,1)S(1)} %collective-permute-done.1.after_ref, ...), custom_call_target="tpu_custom_call" | custom-call | tf_op jit(solution)/shard_map/pallas_call | solution.py:219
  14.3 0.7 broadcast_in_dim.9
  15.0 17.6 %all-to-all-start = ((bf16[32,16,128]{2,1,0:T(8,128)(2,1)}), bf16[32,16,128]{2,1,0:T(8,128)(2,1)S(1)}, u32[]{:S(2)}, u32[]{:S(2)}) async-start(bf16[32,16,128]{2,1,0:T(8,128)(2,1)} %broadcast_in_dim.9), calls=%async_computation | async-start | bytes 262144 | tf_op jit(solution)/shard_map/all_to_all | solution.py:241
  32.7 14.9 %all-to-all-done = bf16[32,16,128]{2,1,0:T(8,128)(2,1)S(1)} async-done(((bf16[32,16,128]{2,1,0:T(8,128)(2,1)}), bf16[32,16,128]{2,1,0:T(8,128)(2,1)S(1)}, u32[]{:S(2)}, u32[]{:S(2)}) %all-to-all-start) | async-done | bytes 131104 | tf_op jit(solution)/shard_map/all_to_all | solution.py:241
  47.6 0.1 broadcast_in_dim.11
  47.7 1.1 %pad_maximum_fusion.1 = bf16[4,1088,128]{2,1,0:T(8,128)(2,1)} fusion(bf16[4,64,128]{2,1,0:T(8,128)(2,1)S(1)} %get-tuple-element.17, bf16[4,1024,128]{2,1,0:T(8,128)(2,1)S(1)} %broadcast_in_dim.11), kind=kLoop, calls=%fused_computation.2 | loop fusion | flops 2228224 | bytes 2228224 | tf_op jit(solution)/shard_map/concatenate | solution.py:256
  48.8 4.2 %all-to-all-start.2 = ((bf16[4,1088,128]{2,1,0:T(8,128)(2,1)}), bf16[4,1088,128]{2,1,0:T(8,128)(2,1)S(1)}, u32[]{:S(2)}, u32[]{:S(2)}) async-start(bf16[4,1088,128]{2,1,0:T(8,128)(2,1)} %pad_maximum_fusion.1), calls=%async_computation.2 | async-start | bytes 2228224 | tf_op jit(solution)/shard_map/all_to_all | solution.py:257
  53.0 1.9 %collective-permute-start.2 = (bf16[1280,128]{1,0:T(8,128)(2,1)S(1)}, bf16[1280,128]{1,0:T(8,128)(2,1)S(1)}, u32[]{:S(2)}, u32[]{:S(2)}) collective-permute-start(bf16[1280,128]{1,0:T(8,128)(2,1)S(1)} %pad_maximum_fusion.2), channel_id=1, source_target_pairs={{0,64},{32,96},{64,0},{96,32},{128,192},{160,224},{192,128},{224,1... | collective-permute-start | bytes 983048 | tf_op jit(solution)/shard_map/ppermute | solution.py:252
  54.9 9.4 %collective-permute-done.2 = bf16[1280,128]{1,0:T(8,128)(2,1)S(1)} collective-permute-done((bf16[1280,128]{1,0:T(8,128)(2,1)S(1)}, bf16[1280,128]{1,0:T(8,128)(2,1)S(1)}, u32[]{:S(2)}, u32[]{:S(2)}) %collective-permute-start.2) | collective-permute-done | bytes 327712 | tf_op jit(solution)/shard_map/ppermute | solution.py:252
  64.3 0.1 broadcast_in_dim.10
  64.5 1.1 %pad_maximum_fusion = bf16[4,1088,128]{2,1,0:T(8,128)(2,1)} fusion(bf16[4,64,128]{2,1,0:T(8,128)(2,1)S(1)} %bitcast.14, bf16[4,1024,128]{2,1,0:T(8,128)(2,1)S(1)} %broadcast_in_dim.10), kind=kLoop, calls=%fused_computation.1 | loop fusion | flops 2228224 | bytes 2228224 | tf_op jit(solution)/shard_map/concatenate | solution.py:256
  65.5 2.8 %all-to-all-done.2.white_ref = bf16[4,1088,128]{2,1,0:T(8,128)(2,1)S(1)} async-done(((bf16[4,1088,128]{2,1,0:T(8,128)(2,1)}), bf16[4,1088,128]{2,1,0:T(8,128)(2,1)S(1)}, u32[]{:S(2)}, u32[]{:S(2)}) %all-to-all-start.2) | async-done | bytes 1114144 | tf_op jit(solution)/shard_map/all_to_all | solution.py:257
  68.4 3.7 %all-to-all-start.1 = ((bf16[4,1088,128]{2,1,0:T(8,128)(2,1)}), bf16[4,1088,128]{2,1,0:T(8,128)(2,1)S(1)}, u32[]{:S(2)}, u32[]{:S(2)}) async-start(bf16[4,1088,128]{2,1,0:T(8,128)(2,1)} %pad_maximum_fusion), calls=%async_computation.1 | async-start | bytes 2228224 | tf_op jit(solution)/shard_map/all_to_all | solution.py:257
  72.1 8.6 %shard_map.29 = (bf16[2048,256]{1,0:T(8,128)(2,1)S(1)}, bf16[2048,256]{1,0:T(8,128)(2,1)S(1)}) custom-call(s32[1]{0:T(128)} %bitcast.5.half_ref, bf16[4,1088,128]{2,1,0:T(8,128)(2,1)S(1)} %all-to-all-done.2.white_ref, f32[4,64,128]{2,1,0:T(8,128)S(1)} %slice_convert_fusion.src_ref), custom_call_target="tpu_custom_call" | custom-call | tf_op jit(solution)/shard_map/pallas_call | solution.py:191
  80.7 0.0 copy-start
  80.7 1.0 copy-done
  81.6 6.1 %all-to-all-done.1.white_ref = bf16[4,1088,128]{2,1,0:T(8,128)(2,1)S(1)} async-done(((bf16[4,1088,128]{2,1,0:T(8,128)(2,1)}), bf16[4,1088,128]{2,1,0:T(8,128)(2,1)S(1)}, u32[]{:S(2)}, u32[]{:S(2)}) %all-to-all-start.1) | async-done | bytes 1114144 | tf_op jit(solution)/shard_map/all_to_all | solution.py:257
  87.8 0.0 copy-start.1
  87.8 1.2 %copy-done.1 = bf16[2048,256]{1,0:T(8,128)(2,1)S(1)} copy-done((bf16[2048,256]{1,0:T(8,128)(2,1)S(1)}, bf16[2048,256]{1,0:T(8,128)(2,1)}, u32[]{:S(2)}) %copy-start.1) | copy-done | bytes 1048600
  89.0 5.9 %shard_map.31 = bf16[4096,128]{1,0:T(8,128)(2,1)S(1)} custom-call(s32[1]{0:T(128)} %bitcast.5.half_ref, bf16[4,1088,128]{2,1,0:T(8,128)(2,1)S(1)} %all-to-all-done.1.white_ref, f32[4,64,128]{2,1,0:T(8,128)S(1)} %slice_convert_fusion.1.src_ref, bf16[2048,256]{1,0:T(8,128)(2,1)S(1)} %copy-done.1), custom_call_target="tpu_custom_call" | custom-call | tf_op jit(solution)/shard_map/pallas_call | solution.py:191
  94.9 2.8 %collective-permute-start.3 = (bf16[4096,128]{1,0:T(8,128)(2,1)S(1)}, bf16[4096,128]{1,0:T(8,128)(2,1)S(1)}, u32[]{:S(2)}, u32[]{:S(2)}) collective-permute-start(bf16[4096,128]{1,0:T(8,128)(2,1)S(1)} %shard_map.31), channel_id=1, source_target_pairs={{0,32},{32,0},{64,96},{96,64},{128,160},{160,128},{192,224},{224,1... | collective-permute-start | bytes 3145736 | tf_op jit(solution)/shard_map/ppermute | solution.py:271
  97.6 5.6 %shard_map.30 = f32[4096,128]{1,0:T(8,128)S(1)} custom-call(s32[1]{0:T(128)} %bitcast.1.half_ref, bf16[4,1088,128]{2,1,0:T(8,128)(2,1)S(1)} %all-to-all-done.1.white_ref, f32[4,64,128]{2,1,0:T(8,128)S(1)} %slice_convert_fusion.1.src_ref, bf16[2048,256]{1,0:T(8,128)(2,1)S(1)} %get-tuple-element.15.refs_0_), custom_call_target="tpu_custom_call" | custom-call | tf_op jit(solution)/shard_map/pallas_call | solution.py:191
  103.2 0.0 collective-permute-done.3
  103.2 1.6 %convert_add_fusion = f32[4096,128]{1,0:T(8,128)} fusion(f32[4096,128]{1,0:T(8,128)S(1)} %shard_map.30, bf16[4096,128]{1,0:T(8,128)(2,1)S(1)} %collective-permute-done.3), kind=kLoop, calls=%fused_computation | loop fusion | flops 1048576 | bytes 5242880 | tf_op jit(solution)/shard_map/add | solution.py:273
  (6 shorter events, 0.1 us)
Async XLA Ops:
  0.0 10.9 %collective-permute-start = (bf16[1024,128]{1,0:T(8,128)(2,1)}, bf16[1024,128]{1,0:T(8,128)(2,1)S(1)}, u32[]{:S(2)}, u32[]{:S(2)}) collective-permute-start(bf16[1024,128]{1,0:T(8,128)(2,1)} %raw_ref.1), channel_id=1, source_target_pairs={{0,32},{32,64},{64,96},{96,128},{128,160},{160,192},{192,224},{224... | collective-permute-start | bytes 786440 | tf_op jit(solution)/shard_map/ppermute | solution.py:214
  4.8 6.1 %collective-permute-start.1 = (bf16[128,128]{1,0:T(8,128)(2,1)S(1)}, bf16[128,128]{1,0:T(8,128)(2,1)S(1)}, u32[]{:S(2)}, u32[]{:S(2)}) collective-permute-start(bf16[128,128]{1,0:T(8,128)(2,1)S(1)} %slice.17), channel_id=1, source_target_pairs={{32,0},{64,32},{96,64},{128,96},{160,128},{192,160},{224,192},{256... | collective-permute-start | bytes 98312 | tf_op jit(solution)/shard_map/ppermute | solution.py:215
  10.9 1.0 copy-start.2
  15.0 32.6 %all-to-all-start = ((bf16[32,16,128]{2,1,0:T(8,128)(2,1)}), bf16[32,16,128]{2,1,0:T(8,128)(2,1)S(1)}, u32[]{:S(2)}, u32[]{:S(2)}) async-start(bf16[32,16,128]{2,1,0:T(8,128)(2,1)} %broadcast_in_dim.9), calls=%async_computation | async-start | bytes 262144 | tf_op jit(solution)/shard_map/all_to_all | solution.py:241
  48.8 19.6 %all-to-all-start.2 = ((bf16[4,1088,128]{2,1,0:T(8,128)(2,1)}), bf16[4,1088,128]{2,1,0:T(8,128)(2,1)S(1)}, u32[]{:S(2)}, u32[]{:S(2)}) async-start(bf16[4,1088,128]{2,1,0:T(8,128)(2,1)} %pad_maximum_fusion.1), calls=%async_computation.2 | async-start | bytes 2228224 | tf_op jit(solution)/shard_map/all_to_all | solution.py:257
  53.0 11.3 %collective-permute-start.2 = (bf16[1280,128]{1,0:T(8,128)(2,1)S(1)}, bf16[1280,128]{1,0:T(8,128)(2,1)S(1)}, u32[]{:S(2)}, u32[]{:S(2)}) collective-permute-start(bf16[1280,128]{1,0:T(8,128)(2,1)S(1)} %pad_maximum_fusion.2), channel_id=1, source_target_pairs={{0,64},{32,96},{64,0},{96,32},{128,192},{160,224},{192,128},{224,1... | collective-permute-start | bytes 983048 | tf_op jit(solution)/shard_map/ppermute | solution.py:252
  68.4 19.4 %all-to-all-start.1 = ((bf16[4,1088,128]{2,1,0:T(8,128)(2,1)}), bf16[4,1088,128]{2,1,0:T(8,128)(2,1)S(1)}, u32[]{:S(2)}, u32[]{:S(2)}) async-start(bf16[4,1088,128]{2,1,0:T(8,128)(2,1)} %pad_maximum_fusion), calls=%async_computation.1 | async-start | bytes 2228224 | tf_op jit(solution)/shard_map/all_to_all | solution.py:257
  80.7 1.0 copy-start
  87.8 1.2 %copy-start.1 = (bf16[2048,256]{1,0:T(8,128)(2,1)S(1)}, bf16[2048,256]{1,0:T(8,128)(2,1)}, u32[]{:S(2)}) copy-start(bf16[2048,256]{1,0:T(8,128)(2,1)} %copy-done) | copy-start | bytes 3145732
  94.9 8.3 %collective-permute-start.3 = (bf16[4096,128]{1,0:T(8,128)(2,1)S(1)}, bf16[4096,128]{1,0:T(8,128)(2,1)S(1)}, u32[]{:S(2)}, u32[]{:S(2)}) collective-permute-start(bf16[4096,128]{1,0:T(8,128)(2,1)S(1)} %shard_map.31), channel_id=1, source_target_pairs={{0,32},{32,0},{64,96},{96,64},{128,160},{160,128},{192,224},{224,1... | collective-permute-start | bytes 3145736 | tf_op jit(solution)/shard_map/ppermute | solution.py:271

commit v5 on v4

--- a/solution.py
+++ b/solution.py
@@ -238,32 +238,36 @@
         ],
         compiler_params=pltpu.CompilerParams(vmem_limit_bytes=50 << 20),
     )(last, before, raw, after, taps[None])
+    lines = chips // 2
+    near_side = (place // 2 % 2).astype(F32)
+    own = core.reshape(1)
+    other = (1 - core).reshape(1)
+    src, near_side, own, other = lax.optimization_barrier((src, near_side, own, other))
     every = lax.all_to_all(
         jnp.broadcast_to(src[None], (chan_parts,) + src.shape), "chan", 0, 0, tiled=True
     )
-    lines = chips // 2
-    place, white, _ = lax.optimization_barrier((place, white, every[0, 0, 0]))
-    core = place % 2
-    side = place // 2 % 2
     every = every.reshape(lines, 2, sources * frame_rows, 128)
-    mine = lax.dynamic_index_in_dim(every, side, 1, keepdims=False)
-    others = lax.dynamic_index_in_dim(every, 1 - side, 1, keepdims=False)
+    white, every = lax.optimization_barrier((white, every))
+    second = near_side > 0.5
+    mine = jnp.where(second, every[:, 1], every[:, 0])
+    others = jnp.where(second, every[:, 0], every[:, 1])
     far = jnp.concatenate([white, others.reshape(-1, 128)], 0)
-    far = lax.ppermute(far, "tm", [(i, i ^ 2) for i in range(time_parts)])
     groups = [[c + 4 * i for i in range(lines)] for c in range(4)]
 
-    def gather(frame, srcs):
-        both = jnp.concatenate([jnp.broadcast_to(frame[None], (lines,) + frame.shape), srcs], 1)
-        return lax.all_to_all(both, "tm", 0, 0, tiled=True, axis_index_groups=groups)
+    def bundled(frame, srcs):
+        return jnp.concatenate([jnp.broadcast_to(frame[None], (lines,) + frame.shape), srcs], 1)
+
+    def gather(bundle):
+        return lax.all_to_all(bundle, "tm", 0, 0, tiled=True, axis_index_groups=groups)
 
     def signals(bundle):
         return bundle[:, frame_rows * channels :].astype(F32)
 
-    near = gather(white, mine)
-    far = lax.optimization_barrier((far, near[0, 0, 0]))[0]
-    far = gather(far[: white.shape[0]], far[white.shape[0] :].reshape(mine.shape))
-    other = (1 - core).reshape(1)
-    own = core.reshape(1)
+    near, far = lax.optimization_barrier((bundled(white, mine), far))
+    far = lax.ppermute(far, "tm", [(i, i ^ 2) for i in range(time_parts)])
+    near = gather(near)
+    far = bundled(far[: white.shape[0]], far[white.shape[0] :].reshape(mine.shape))
+    far = gather(lax.optimization_barrier((far, near[0, 0, 0]))[0])
     parts = correlate(other, near, signals(near), channels, scale, sources)
     half = sources // 2
     srcs = signals(far)

time: 105 us -> 105 us (level)
  no operation moved by 1% of the time
where the time goes in v5:
time: 105 us
  waiting for transfers between devices  36.7 us (35%)
  starting transfers between devices  36.1 us (34%)
  Pallas kernels  22.4 us (21%)
  local copies, waits for them, and re-layouts  5.59 us (5%)
  other arithmetic  3.77 us (4%)
    pallas_call x3, Pallas kernels, correlate(): pl.pallas_call(functools.partial(correlate_kernel, scale=scale, count=cou...  20 us
    all_to_all x1, starting transfers between devices, on_device(): lax.all_to_all(jnp.broadcast_to(src[None], (chan_parts,) + src.shape), 'c...  17.6 us
    all_to_all x1, waiting for transfers between devices, on_device(): lax.all_to_all(jnp.broadcast_to(src[None], (chan_parts,) + src.shape), 'c...  14.9 us
    ppermute x1, waiting for transfers between devices, on_device(): far = lax.ppermute(far, 'tm', [(i, i ^ 2) for i in range(time_parts)])  9.37 us
    all_to_all x2, waiting for transfers between devices, gather(): lax.all_to_all(bundle, 'tm', 0, 0, tiled=True, axis_index_groups=groups)  8.97 us
    all_to_all x2, starting transfers between devices, gather(): lax.all_to_all(bundle, 'tm', 0, 0, tiled=True, axis_index_groups=groups)  7.88 us
    ppermute x1, starting transfers between devices, on_device(): before = lax.ppermute(raw, 'tm', up)  4.02 us
    ppermute x1, waiting for transfers between devices, on_device(): after = lax.ppermute(raw[:AFTER], 'tm', down)  3.48 us
  transfers between devices with their start and end apart: 7, of which 5 were waited for; matrix products, arithmetic and copies ran while one was open for 3% of the time, Pallas kernels for 13%

profile of v5, /device:TPU:7, one launch (start us, length us, event | category | flops | bytes accessed | tf_op | source)
XLA Modules:
  0.0 104.8 jit_solution(7507631242342688679)
XLA Ops:
  0.0 4.0 %collective-permute-start = (bf16[1024,128]{1,0:T(8,128)(2,1)}, bf16[1024,128]{1,0:T(8,128)(2,1)S(1)}, u32[]{:S(2)}, u32[]{:S(2)}) collective-permute-start(bf16[1024,128]{1,0:T(8,128)(2,1)} %raw_ref.1), channel_id=1, source_target_pairs={{0,32},{32,64},{64,96},{96,128},{128,160},{160,192},{192,224},{224... | collective-permute-start | bytes 786440 | tf_op jit(solution)/shard_map/ppermute | solution.py:214
  4.0 0.8 slice.24
  4.8 1.9 %collective-permute-start.1 = (bf16[128,128]{1,0:T(8,128)(2,1)S(1)}, bf16[128,128]{1,0:T(8,128)(2,1)S(1)}, u32[]{:S(2)}, u32[]{:S(2)}) collective-permute-start(bf16[128,128]{1,0:T(8,128)(2,1)S(1)} %slice.24), channel_id=1, source_target_pairs={{32,0},{64,32},{96,64},{128,96},{160,128},{192,160},{224,192},{256... | collective-permute-start | bytes 98312 | tf_op jit(solution)/shard_map/ppermute | solution.py:215
  6.8 0.7 broadcast_in_dim.8.taps_ref
  7.4 3.5 %collective-permute-done.1.after_ref = bf16[128,128]{1,0:T(8,128)(2,1)S(1)} collective-permute-done((bf16[128,128]{1,0:T(8,128)(2,1)S(1)}, bf16[128,128]{1,0:T(8,128)(2,1)S(1)}, u32[]{:S(2)}, u32[]{:S(2)}) %collective-permute-start.1) | collective-permute-done | bytes 32800 | tf_op jit(solution)/shard_map/ppermute | solution.py:215
  10.9 0.0 collective-permute-done.before_ref
  10.9 0.0 copy-start.2
  10.9 0.9 copy-done.2
  11.9 2.4 %shard_map.28 = (bf16[1024,128]{1,0:T(8,128)(2,1)S(1)}, bf16[16,128]{1,0:T(8,128)(2,1)S(1)}) custom-call(s32[1]{0:T(128)} %bitcast.last_ref, bf16[1024,128]{1,0:T(8,128)(2,1)S(1)} %collective-permute-done.before_ref, bf16[1024,128]{1,0:T(8,128)(2,1)S(1)} %copy-done.2, bf16[128,128]{1,0:T(8,128)(2,1)S(1)} %collective-permute-done.1.after_ref, ...), custom_call_target="tpu_custom_call" | custom-call | tf_op jit(solution)/shard_map/pallas_call | solution.py:219
  14.3 0.7 broadcast_in_dim.9
  15.0 17.6 %all-to-all-start = ((bf16[32,16,128]{2,1,0:T(8,128)(2,1)}), bf16[32,16,128]{2,1,0:T(8,128)(2,1)S(1)}, u32[]{:S(2)}, u32[]{:S(2)}) async-start(bf16[32,16,128]{2,1,0:T(8,128)(2,1)} %broadcast_in_dim.9), calls=%async_computation | async-start | bytes 262144 | tf_op jit(solution)/shard_map/all_to_all | solution.py:246
  32.6 14.9 %all-to-all-done = bf16[32,16,128]{2,1,0:T(8,128)(2,1)S(1)} async-done(((bf16[32,16,128]{2,1,0:T(8,128)(2,1)}), bf16[32,16,128]{2,1,0:T(8,128)(2,1)S(1)}, u32[]{:S(2)}, u32[]{:S(2)}) %all-to-all-start) | async-done | bytes 131104 | tf_op jit(solution)/shard_map/all_to_all | solution.py:246
  47.6 0.1 broadcast_in_dim.10
  47.8 1.1 %pad_maximum_fusion = bf16[4,1088,128]{2,1,0:T(8,128)(2,1)} fusion(bf16[4,64,128]{2,1,0:T(8,128)(2,1)S(1)} %get-tuple-element.30, bf16[4,1024,128]{2,1,0:T(8,128)(2,1)S(1)} %broadcast_in_dim.10), kind=kLoop, calls=%fused_computation.1 | loop fusion | flops 2228224 | bytes 2228224 | tf_op jit(solution)/shard_map/concatenate | solution.py:258
  48.8 4.2 %all-to-all-start.2 = ((bf16[4,1088,128]{2,1,0:T(8,128)(2,1)}), bf16[4,1088,128]{2,1,0:T(8,128)(2,1)S(1)}, u32[]{:S(2)}, u32[]{:S(2)}) async-start(bf16[4,1088,128]{2,1,0:T(8,128)(2,1)} %pad_maximum_fusion), calls=%async_computation.2 | async-start | bytes 2228224 | tf_op jit(solution)/shard_map/all_to_all | solution.py:261
  53.0 1.9 %collective-permute-start.2 = (bf16[1280,128]{1,0:T(8,128)(2,1)S(1)}, bf16[1280,128]{1,0:T(8,128)(2,1)S(1)}, u32[]{:S(2)}, u32[]{:S(2)}) collective-permute-start(bf16[1280,128]{1,0:T(8,128)(2,1)S(1)} %pad_maximum_fusion.2), channel_id=1, source_target_pairs={{0,64},{32,96},{64,0},{96,32},{128,192},{160,224},{192,128},{224,1... | collective-permute-start | bytes 983048 | tf_op jit(solution)/shard_map/ppermute | solution.py:267
  54.9 9.4 %collective-permute-done.2 = bf16[1280,128]{1,0:T(8,128)(2,1)S(1)} collective-permute-done((bf16[1280,128]{1,0:T(8,128)(2,1)S(1)}, bf16[1280,128]{1,0:T(8,128)(2,1)S(1)}, u32[]{:S(2)}, u32[]{:S(2)}) %collective-permute-start.2) | collective-permute-done | bytes 327712 | tf_op jit(solution)/shard_map/ppermute | solution.py:267
  64.3 0.1 broadcast_in_dim.11
  64.5 1.1 %pad_maximum_fusion.1 = bf16[4,1088,128]{2,1,0:T(8,128)(2,1)} fusion(bf16[4,64,128]{2,1,0:T(8,128)(2,1)S(1)} %bitcast.14, bf16[4,1024,128]{2,1,0:T(8,128)(2,1)S(1)} %broadcast_in_dim.11), kind=kLoop, calls=%fused_computation.2 | loop fusion | flops 2228224 | bytes 2228224 | tf_op jit(solution)/shard_map/concatenate | solution.py:258
  65.6 2.8 %all-to-all-done.2.white_ref = bf16[4,1088,128]{2,1,0:T(8,128)(2,1)S(1)} async-done(((bf16[4,1088,128]{2,1,0:T(8,128)(2,1)}), bf16[4,1088,128]{2,1,0:T(8,128)(2,1)S(1)}, u32[]{:S(2)}, u32[]{:S(2)}) %all-to-all-start.2) | async-done | bytes 1114144 | tf_op jit(solution)/shard_map/all_to_all | solution.py:261
  68.4 3.7 %all-to-all-start.1 = ((bf16[4,1088,128]{2,1,0:T(8,128)(2,1)}), bf16[4,1088,128]{2,1,0:T(8,128)(2,1)S(1)}, u32[]{:S(2)}, u32[]{:S(2)}) async-start(bf16[4,1088,128]{2,1,0:T(8,128)(2,1)} %pad_maximum_fusion.1), calls=%async_computation.1 | async-start | bytes 2228224 | tf_op jit(solution)/shard_map/all_to_all | solution.py:261
  72.1 8.6 %shard_map.29 = (bf16[2048,256]{1,0:T(8,128)(2,1)S(1)}, bf16[2048,256]{1,0:T(8,128)(2,1)S(1)}) custom-call(s32[1]{0:T(128)} %bitcast.2.half_ref, bf16[4,1088,128]{2,1,0:T(8,128)(2,1)S(1)} %all-to-all-done.2.white_ref, f32[4,64,128]{2,1,0:T(8,128)S(1)} %slice_convert_fusion.src_ref), custom_call_target="tpu_custom_call" | custom-call | tf_op jit(solution)/shard_map/pallas_call | solution.py:191
  80.7 0.0 copy-start
  80.7 1.0 copy-done
  81.7 6.1 %all-to-all-done.1.white_ref = bf16[4,1088,128]{2,1,0:T(8,128)(2,1)S(1)} async-done(((bf16[4,1088,128]{2,1,0:T(8,128)(2,1)}), bf16[4,1088,128]{2,1,0:T(8,128)(2,1)S(1)}, u32[]{:S(2)}, u32[]{:S(2)}) %all-to-all-start.1) | async-done | bytes 1114144 | tf_op jit(solution)/shard_map/all_to_all | solution.py:261
  87.8 0.0 copy-start.1
  87.8 1.2 %copy-done.1 = bf16[2048,256]{1,0:T(8,128)(2,1)S(1)} copy-done((bf16[2048,256]{1,0:T(8,128)(2,1)S(1)}, bf16[2048,256]{1,0:T(8,128)(2,1)}, u32[]{:S(2)}) %copy-start.1) | copy-done | bytes 1048600
  89.1 5.9 %shard_map.31 = bf16[4096,128]{1,0:T(8,128)(2,1)S(1)} custom-call(s32[1]{0:T(128)} %bitcast.2.half_ref, bf16[4,1088,128]{2,1,0:T(8,128)(2,1)S(1)} %all-to-all-done.1.white_ref, f32[4,64,128]{2,1,0:T(8,128)S(1)} %slice_convert_fusion.1.src_ref, bf16[2048,256]{1,0:T(8,128)(2,1)S(1)} %copy-done.1), custom_call_target="tpu_custom_call" | custom-call | tf_op jit(solution)/shard_map/pallas_call | solution.py:191
  94.9 2.8 %collective-permute-start.3 = (bf16[4096,128]{1,0:T(8,128)(2,1)S(1)}, bf16[4096,128]{1,0:T(8,128)(2,1)S(1)}, u32[]{:S(2)}, u32[]{:S(2)}) collective-permute-start(bf16[4096,128]{1,0:T(8,128)(2,1)S(1)} %shard_map.31), channel_id=1, source_target_pairs={{0,32},{32,0},{64,96},{96,64},{128,160},{160,128},{192,224},{224,1... | collective-permute-start | bytes 3145736 | tf_op jit(solution)/shard_map/ppermute | solution.py:275
  97.7 5.6 %shard_map.30 = f32[4096,128]{1,0:T(8,128)S(1)} custom-call(s32[1]{0:T(128)} %bitcast.1.half_ref, bf16[4,1088,128]{2,1,0:T(8,128)(2,1)S(1)} %all-to-all-done.1.white_ref, f32[4,64,128]{2,1,0:T(8,128)S(1)} %slice_convert_fusion.1.src_ref, bf16[2048,256]{1,0:T(8,128)(2,1)S(1)} %get-tuple-element.27.refs_0_), custom_call_target="tpu_custom_call" | custom-call | tf_op jit(solution)/shard_map/pallas_call | solution.py:191
  103.3 0.0 collective-permute-done.3
  103.3 1.6 %convert_add_fusion = f32[4096,128]{1,0:T(8,128)} fusion(f32[4096,128]{1,0:T(8,128)S(1)} %shard_map.30, bf16[4096,128]{1,0:T(8,128)(2,1)S(1)} %collective-permute-done.3), kind=kLoop, calls=%fused_computation | loop fusion | flops 1048576 | bytes 5242880 | tf_op jit(solution)/shard_map/add | solution.py:277
  (6 shorter events, 0.1 us)
Async XLA Ops:
  0.0 10.9 %collective-permute-start = (bf16[1024,128]{1,0:T(8,128)(2,1)}, bf16[1024,128]{1,0:T(8,128)(2,1)S(1)}, u32[]{:S(2)}, u32[]{:S(2)}) collective-permute-start(bf16[1024,128]{1,0:T(8,128)(2,1)} %raw_ref.1), channel_id=1, source_target_pairs={{0,32},{32,64},{64,96},{96,128},{128,160},{160,192},{192,224},{224... | collective-permute-start | bytes 786440 | tf_op jit(solution)/shard_map/ppermute | solution.py:214
  4.8 6.1 %collective-permute-start.1 = (bf16[128,128]{1,0:T(8,128)(2,1)S(1)}, bf16[128,128]{1,0:T(8,128)(2,1)S(1)}, u32[]{:S(2)}, u32[]{:S(2)}) collective-permute-start(bf16[128,128]{1,0:T(8,128)(2,1)S(1)} %slice.24), channel_id=1, source_target_pairs={{32,0},{64,32},{96,64},{128,96},{160,128},{192,160},{224,192},{256... | collective-permute-start | bytes 98312 | tf_op jit(solution)/shard_map/ppermute | solution.py:215
  10.9 1.0 copy-start.2
  15.0 32.6 %all-to-all-start = ((bf16[32,16,128]{2,1,0:T(8,128)(2,1)}), bf16[32,16,128]{2,1,0:T(8,128)(2,1)S(1)}, u32[]{:S(2)}, u32[]{:S(2)}) async-start(bf16[32,16,128]{2,1,0:T(8,128)(2,1)} %broadcast_in_dim.9), calls=%async_computation | async-start | bytes 262144 | tf_op jit(solution)/shard_map/all_to_all | solution.py:246
  48.8 19.6 %all-to-all-start.2 = ((bf16[4,1088,128]{2,1,0:T(8,128)(2,1)}), bf16[4,1088,128]{2,1,0:T(8,128)(2,1)S(1)}, u32[]{:S(2)}, u32[]{:S(2)}) async-start(bf16[4,1088,128]{2,1,0:T(8,128)(2,1)} %pad_maximum_fusion), calls=%async_computation.2 | async-start | bytes 2228224 | tf_op jit(solution)/shard_map/all_to_all | solution.py:261
  53.0 11.3 %collective-permute-start.2 = (bf16[1280,128]{1,0:T(8,128)(2,1)S(1)}, bf16[1280,128]{1,0:T(8,128)(2,1)S(1)}, u32[]{:S(2)}, u32[]{:S(2)}) collective-permute-start(bf16[1280,128]{1,0:T(8,128)(2,1)S(1)} %pad_maximum_fusion.2), channel_id=1, source_target_pairs={{0,64},{32,96},{64,0},{96,32},{128,192},{160,224},{192,128},{224,1... | collective-permute-start | bytes 983048 | tf_op jit(solution)/shard_map/ppermute | solution.py:267
  68.4 19.4 %all-to-all-start.1 = ((bf16[4,1088,128]{2,1,0:T(8,128)(2,1)}), bf16[4,1088,128]{2,1,0:T(8,128)(2,1)S(1)}, u32[]{:S(2)}, u32[]{:S(2)}) async-start(bf16[4,1088,128]{2,1,0:T(8,128)(2,1)} %pad_maximum_fusion.1), calls=%async_computation.1 | async-start | bytes 2228224 | tf_op jit(solution)/shard_map/all_to_all | solution.py:261
  80.7 1.0 copy-start
  87.8 1.2 %copy-start.1 = (bf16[2048,256]{1,0:T(8,128)(2,1)S(1)}, bf16[2048,256]{1,0:T(8,128)(2,1)}, u32[]{:S(2)}) copy-start(bf16[2048,256]{1,0:T(8,128)(2,1)} %copy-done) | copy-start | bytes 3145732
  94.9 8.3 %collective-permute-start.3 = (bf16[4096,128]{1,0:T(8,128)(2,1)S(1)}, bf16[4096,128]{1,0:T(8,128)(2,1)S(1)}, u32[]{:S(2)}, u32[]{:S(2)}) collective-permute-start(bf16[4096,128]{1,0:T(8,128)(2,1)S(1)} %shard_map.31), channel_id=1, source_target_pairs={{0,32},{32,0},{64,96},{96,64},{128,160},{160,128},{192,224},{224,1... | collective-permute-start | bytes 3145736 | tf_op jit(solution)/shard_map/ppermute | solution.py:275
